TPU v7x, 32 devices: a whole 2x2x4 slice. The times are simulated.
32 devices in a mesh: dp: 4 (over y, core), tensor: 8 (over z, x).
Axes of the slice: x: 2, y: 2, z: 4, core: 2. Of those that a mesh axis runs over, the one named last changes fastest.
Arguments:
- inputs: bfloat16 [16384, 28672], P('dp', 'tensor'), may hold values from -6 to 6
- out_grads: bfloat16 [16384, 8192], P('dp', 'tensor'), may hold values from -6 to 6
- proj_in: bfloat16 [28672, 64], P('tensor'), may hold values from -0.03125 to 0.03125
- proj_out: bfloat16 [8192, 64], P('tensor'), may hold values from -0.0625 to 0.0625
- lengths: int32 [16], replicated, may hold values from 1 to 4096, 16384 in all
- valid_feats: bfloat16 [4096, 4096], P('dp', 'tensor'), may hold values from -6 to 6
Outputs:
- scores: float32 [16, 4096], P(None, ('dp', 'tensor'))
Inputs may be any that keep to these rules, and one draw needn't show every extreme that they name: The lengths sum to 16384; the largest is exactly 4096.
All inputs are finite; a program needn't handle non-finite values.
Results may differ from a plain program's by a relative error of at most 0.003.
Values sent between devices are 32-bit elements; how exact they have to be, the bound alone decides.
No kernel may reach another device: no remote copies, remote signals or barrier semaphores. Data moves between devices by JAX's collectives and lax.ppermute only.
A program may use at most 128 MiB of HBM per device.

v0:
```python
import jax
import jax.numpy as jnp
from jax import lax
from jax.sharding import PartitionSpec as P


def member_rows(positions, prompt_starts, prompt_ends):
    inside = (positions[None, :] >= prompt_starts[:, None]) & (
        positions[None, :] < prompt_ends[:, None]
    )
    return inside.astype(jnp.float32)


def outer_sums(members, grad_rows, act_rows):
    return jnp.einsum(
        "pt,ti,tj->pij", members, grad_rows, act_rows, precision=lax.Precision.HIGHEST
    )


def shards(inputs, out_grads, proj_in, proj_out, lengths, valid_feats):
    tok_rows = inputs.shape[0]
    proj_rank = proj_in.shape[1]
    prompt_count = lengths.shape[0]
    act_part = jnp.dot(inputs, proj_in, preferred_element_type=jnp.float32)
    grad_part = jnp.dot(out_grads, proj_out, preferred_element_type=jnp.float32)
    paired = jnp.concatenate([act_part, grad_part], axis=1)
    prompt_ends = jnp.cumsum(lengths)
    prompt_starts = prompt_ends - lengths
    tensor_count = lax.axis_size("tensor")
    tensor_pos = lax.axis_index("tensor")
    slice_width = proj_rank * proj_rank // tensor_count
    first_row = lax.axis_index("dp") * tok_rows
    summed_pair = lax.psum(paired, "tensor")
    row_count = proj_rank // tensor_count
    grad_rows = lax.dynamic_slice_in_dim(
        summed_pair[:, proj_rank:], tensor_pos * row_count, row_count, 1
    )
    positions = first_row + jnp.arange(tok_rows, dtype=jnp.int32)
    members = member_rows(positions, prompt_starts, prompt_ends)
    gram_rows = outer_sums(members, grad_rows, summed_pair[:, :proj_rank])
    gram_rows = gram_rows.reshape(prompt_count, slice_width)
    summed = lax.psum(gram_rows, "dp")
    features = (summed / lengths[:, None].astype(jnp.float32)).astype(jnp.bfloat16)
    partial_value = lax.dot_general(
        features, valid_feats, (((1,), (1,)), ((), ())), preferred_element_type=jnp.float32
    )
    return lax.psum_scatter(partial_value, "tensor", scatter_dimension=1, tiled=True)


def solution(mesh):
    return jax.shard_map(
        shards,
        mesh=mesh,
        in_specs=(
            P("dp", "tensor"),
            P("dp", "tensor"),
            P("tensor", None),
            P("tensor", None),
            P(),
            P("dp", "tensor"),
        ),
        out_specs=P(None, ("dp", "tensor")),
        check_vma=False,
    )
```

profile of v0, /device:TPU:0, one launch (start us, length us, event | category | flops | bytes accessed | tf_op | source)
XLA Modules:
  0.0 210.4 jit_solution(1678884307394974821)
XLA Ops:
  6.5 0.0 copy-start
  6.5 0.0 copy-start.1
  6.5 0.0 all-reduce.2.cloned.1.call-start
  6.5 6.2 %fusion.11 = f32[4096,64]{0,1:T(8,128)S(1)} fusion(bf16[4096,1024]{1,0:T(8,128)(2,1)} %param.7, bf16[1024,64]{0,1:T(8,128)(2,1)} %param.9), kind=kOutput, calls=%fused_computation.15 | convolution fusion | flops 536870912 | bytes 9568256 | tf_op jit(solution)/shard_map/dot_general | solution.py:25
  12.7 0.0 copy-done.1
  12.7 14.2 %fusion.10 = f32[4096,64]{0,1:T(8,128)S(1)} fusion(bf16[4096,3584]{1,0:T(8,128)(2,1)} %param.6, bf16[3584,64]{0,1:T(8,128)(2,1)S(1)} %copy-done.1), kind=kOutput, calls=%fused_computation.14 | convolution fusion | flops 1879048192 | bytes 30867456 | tf_op jit(solution)/shard_map/dot_general | solution.py:24
  26.9 1.4 pad_maximum_fusion
  28.3 0.0 copy-start.2
  28.3 0.0 all-reduce.2.cloned.1.call-update
  28.4 0.0 reduce-scatter.2.cloned.1.call-start
  28.4 0.6 copy-done.2
  29.0 0.1 copy.8
  29.1 0.1 reduce
  29.3 0.1 convert_bitcast_fusion
  29.4 104.2 %all-reduce.2.cloned.1.call-done = f32[4096,128]{0,1:T(8,128)} async-done(((f32[4096,128]{0,1:T(8,128)}), f32[4096,128]{0,1:T(8,128)}) %all-reduce.2.cloned.1.call-update) | async-done | bytes 2097168 | tf_op jit(solution)/shard_map/psum | solution.py:33
  133.6 0.0 slice-start
  133.6 1.2 slice-done
  134.8 3.0 %fusion.2 = f32[16,8,64]{2,0,1:T(8,128)S(1)} fusion(f32[4096,128]{0,1:T(8,128)} %all-reduce.2.cloned.1.call-done, f32[4096,16]{0,1:T(8,128)S(1)} %convert_bitcast_fusion, f32[4096,8]{0,1:T(8,128)S(1)} %constant_dynamic-slice_fusion), kind=kOutput, calls=%fused_computation.3 | convolution fusion | flops 403177472 | bytes 1474560 | tf_op jit(solution)/shard_map/pt,ti,tj->pij/dot_general | solution.py:15
  137.8 0.1 reshape.34
  137.9 10.6 %psum.15 = f32[16,512]{1,0:T(8,128)S(1)} all-reduce(f32[16,512]{1,0:T(8,128)S(1)} %reshape.34), channel_id=1, replica_groups=mesh['dp'=4,'tensor'=8] {'dp'}, use_global_device_ids=true, to_apply=%region_2.3 | all-reduce | flops 8192 | bytes 65536 | tf_op jit(solution)/shard_map/psum | solution.py:42
  148.6 0.0 copy-done
  148.6 1.0 fusion.7
  149.6 0.0 reduce-scatter.2.cloned.1.call-update
  149.6 54.0 %reduce-scatter.2.cloned.1.call-done = f32[16,128]{1,0:T(8,128)} async-done(((f32[16,1024]{1,0:T(8,128)}), f32[16,128]{1,0:T(8,128)}) %reduce-scatter.2.cloned.1.call-update) | async-done | bytes 8208 | tf_op jit(solution)/shard_map/reduce_scatter | solution.py:47
  (5 shorter events, 0.1 us)
Async XLA Ops:
  6.5 142.0 %copy-start = (bf16[1024,512]{1,0:T(8,128)(2,1)S(1)}, bf16[1024,512]{1,0:T(8,128)(2,1)}, u32[]{:S(2)}) copy-start(bf16[1024,512]{1,0:T(8,128)(2,1)} %param.11) | copy-start | bytes 3145732
  6.5 6.2 %copy-start.1 = (bf16[3584,64]{0,1:T(8,128)(2,1)S(1)}, bf16[3584,64]{0,1:T(8,128)(2,1)}, u32[]{:S(2)}) copy-start(bf16[3584,64]{0,1:T(8,128)(2,1)} %param.8) | copy-start | bytes 1376260
  6.5 127.0 %all-reduce.2.cloned.1.call-start = ((), (), s32[]{:S(2)}) async-start(), calls=%async_computation.1 | async-start | bytes 4194304 | tf_op jit(solution)/shard_map/psum | solution.py:33
  28.3 0.7 copy-start.2
  28.4 175.2 %reduce-scatter.2.cloned.1.call-start = ((), (), s32[]{:S(2)}) async-start(), calls=%async_computation.2 | async-start | bytes 73728 | tf_op jit(solution)/shard_map/reduce_scatter | solution.py:47
  133.6 1.2 slice-start
Sparse Core Ops, SparseCore 0:
  28.5 105.0 all-reduce.1
  149.7 53.7 reduce-scatter.1
where the time goes:
time: 211 us; the launch traced here: 210 us
  waiting for transfers between devices  158 us (75%)
  matrix products  24.4 us (12%)
  between operations  13.5 us (6%)
  blocking collectives  10.6 us (5%)
    psum x1, waiting for transfers between devices, shards(): summed_pair = lax.psum(paired, 'tensor')  104 us
    reduce_scatter x1, waiting for transfers between devices, shards(): lax.psum_scatter(partial_value, 'tensor', scatter_dimension=1, tiled=True)  54 us
    dot_general x1, matrix products, shards(): act_part = jnp.dot(inputs, proj_in, preferred_element_type=jnp.float32)  14.2 us
    psum x1, blocking collectives, shards(): summed = lax.psum(gram_rows, 'dp')  10.6 us
    dot_general x1, matrix products, shards(): grad_part = jnp.dot(out_grads, proj_out, preferred_element_type=jnp.float32)  6.15 us
  transfers between devices with their start and end apart: 2, of which 2 were waited for; matrix products, arithmetic and copies ran while one was open for 0% of the time, Pallas kernels for 0%

commit v1 on v0

v1 whole, which is shorter than its diff:
```python
import functools
import math

import jax
import jax.numpy as jnp
from jax import lax
from jax.experimental import pallas as pl
from jax.experimental.pallas import tpu as pltpu
from jax.sharding import PartitionSpec as P

NT = (((1,), (1,)), ((), ()))
VMEM_LIMIT = 24 << 20


def dot_nt(a, b):
    return lax.dot_general(a, b, NT, preferred_element_type=jnp.float32)


def lowest(j):
    return (j & -j).bit_length() - 1


def project_kernel(first, final, n_recv, n_blocks, here, after, me, x, g, *refs):
    refs = list(refs)
    ins = [refs.pop(0) for _ in range(2 if first else 4)]
    recvs = [refs.pop(0) for _ in range(n_recv)]
    out = refs.pop(0)
    nexts = [] if final else [refs.pop(0), refs.pop(0)]
    copies, sem = [], refs.pop()

    def rows(at):
        block, size, offset, count = at
        start = (block ^ (me[0] & (n_blocks - 1))) * size + offset
        return pl.ds(pl.multiple_of(start, math.gcd(size, offset, count)), count)

    def fetch(source, target):
        copy = pltpu.make_async_copy(source, target, sem.at[len(copies)])
        copy.start()
        copies.append(copy)

    if first:
        w_in, w_out, x_now, g_now = refs
        fetch(ins[0], w_in)
        fetch(ins[1], w_out)
        fetch(x.at[rows(here)], x_now)
        fetch(g.at[rows(here)], g_now)
    else:
        w_in, w_out, x_now, g_now = ins
    needed = len(copies)
    if not final:
        fetch(x.at[rows(after)], nexts[0])
        fetch(g.at[rows(after)], nexts[1])
    for copy in copies[:needed]:
        copy.wait()
    rank = w_in.shape[0]
    half = rank // 2
    kept = me[0] // n_blocks
    act = dot_nt(w_in[...], x_now[...])
    grad = dot_nt(w_out[...], g_now[...])
    total = jnp.zeros((2 * rank, act.shape[1]), jnp.float32)
    for r in recvs:
        total = total + r[...]
    out[half : half + rank] = act if not recvs else act + total[half : half + rank]
    for h in range(2):
        to = pl.multiple_of(jnp.where(kept == h, half + rank, 0), half)
        line = grad[h * half : (h + 1) * half]
        for r in recvs:
            line = line + r[pl.ds(to, half), :]
        out[pl.ds(to, half), :] = line
    for copy in copies[needed:]:
        copy.wait()


def project(me, x, g, held, recvs, here, after, n_blocks):
    first, final = len(held) == 2, after is None
    vmem = pl.BlockSpec(memory_space=pltpu.VMEM)
    hbm = pl.BlockSpec(memory_space=pltpu.HBM)
    smem = pl.BlockSpec(memory_space=pltpu.SMEM)
    rank = held[0].shape[0]
    wide = (x.shape[1], g.shape[1])
    outs = [pltpu.VMEM((2 * rank, here[3]), jnp.float32)]
    if not final:
        outs += [pltpu.VMEM((after[3], w), jnp.bfloat16) for w in wide]
    if first:
        outs += [pltpu.VMEM(h.shape, h.dtype) for h in held]
    scratch = [pltpu.VMEM((here[3], w), jnp.bfloat16) for w in wide] if first else []
    size = here[3] * sum(wide)
    made = pl.pallas_call(
        functools.partial(project_kernel, first, final, len(recvs), n_blocks, here, after),
        in_specs=[smem, hbm, hbm] + [hbm if first else vmem] * len(held) + [vmem] * len(recvs),
        out_specs=[vmem] * len(outs),
        out_shape=outs,
        scratch_shapes=scratch + [pltpu.SemaphoreType.DMA((6,))],
        name=f"project_{here[0]}_{here[2]}",
        cost_estimate=pl.CostEstimate(flops=4 * rank * size, bytes_accessed=2 * size, transcendentals=0),
        compiler_params=pltpu.CompilerParams(vmem_limit_bytes=VMEM_LIMIT),
    )(me, x, g, *held, *recvs)
    made = list(made)
    if first:
        return made[0], [made[3], made[4], made[1], made[2]]
    return made[0], list(held[:2]) + made[1:]


def gram_kernel(n_blocks, here, tok_rows, has_prev, me, lengths, own, recv, *refs):
    levels = n_blocks.bit_length()
    prevs = refs[:levels] if has_prev else ()
    outs, hi_rows, lo_rows = refs[-levels - 2 : -2], refs[-2], refs[-1]
    half = own.shape[0] // 4
    piece = own.shape[1]
    prompts = lengths.shape[0]
    act = own[half : 3 * half] + recv[half:]
    grad = own[3 * half :] + recv[:half]
    act_hi = act.astype(jnp.bfloat16)
    act_lo = (act - act_hi.astype(jnp.float32)).astype(jnp.bfloat16)
    which = me[0] & (n_blocks - 1)
    first = me[1] * tok_rows + which * here[1] + here[2]
    row = lax.broadcasted_iota(jnp.int32, (prompts, piece), 0)
    position = first + lax.broadcasted_iota(jnp.int32, (prompts, piece), 1)
    begin = jnp.zeros((prompts, piece), jnp.int32)
    end = jnp.zeros((prompts, piece), jnp.int32)
    running = jnp.int32(0)
    for p in range(prompts):
        begin = jnp.where(row == p, running, begin)
        running = running + lengths[p]
        end = jnp.where(row == p, running, end)
    member = (position >= begin) & (position < end)
    for i in range(half):
        line = jnp.broadcast_to(grad[i : i + 1], (prompts, piece))
        line = jnp.where(member, line, 0.0)
        line_hi = line.astype(jnp.bfloat16)
        hi_rows[i * prompts : (i + 1) * prompts] = line_hi
        lo_rows[i * prompts : (i + 1) * prompts] = (line - line_hi.astype(jnp.float32)).astype(jnp.bfloat16)
    width = half * prompts // n_blocks
    for j in range(n_blocks):
        start = pl.multiple_of((j ^ which) * width, width)
        hi = hi_rows[pl.ds(start, width), :]
        lo = lo_rows[pl.ds(start, width), :]
        total = dot_nt(act_hi, hi) + (dot_nt(act_lo, hi) + dot_nt(act_hi, lo))
        level = lowest(j) if j else levels - 1
        at = j >> (level + 1) if j else 0
        if has_prev:
            total = total + prevs[level][at]
        outs[level][at] = total


def gram(me, lengths, own, recv, prevs, here, n_blocks, tok_rows):
    levels = n_blocks.bit_length()
    half = own.shape[0] // 4
    piece = own.shape[1]
    prompts = lengths.shape[0]
    width = half * prompts // n_blocks
    counts = [n_blocks >> (b + 1) for b in range(levels - 1)] + [1]
    vmem = pl.BlockSpec(memory_space=pltpu.VMEM)
    smem = pl.BlockSpec(memory_space=pltpu.SMEM)
    return pl.pallas_call(
        functools.partial(gram_kernel, n_blocks, here, tok_rows, bool(prevs)),
        in_specs=[smem, smem] + [vmem] * (2 + len(prevs)),
        out_specs=[vmem] * levels,
        out_shape=[jax.ShapeDtypeStruct((c, 2 * half, width), jnp.float32) for c in counts],
        scratch_shapes=[pltpu.VMEM((half * prompts, piece), jnp.bfloat16)] * 2,
        name=f"gram_{here[2]}",
        cost_estimate=pl.CostEstimate(
            flops=12 * half * half * prompts * piece, bytes_accessed=8 * own.size, transcendentals=0
        ),
        compiler_params=pltpu.CompilerParams(vmem_limit_bytes=VMEM_LIMIT),
    )(me, lengths, own, recv, *prevs)


def score_kernel(n_ranks, me, lengths, own, recv, valid, *outs):
    levels = n_ranks.bit_length()
    prompts = lengths.shape[0]
    turned = (own[...] + recv[...]).T
    rank = turned.shape[1]
    row = lax.broadcasted_iota(jnp.int32, (prompts, rank), 0)
    count = jnp.ones((prompts, rank), jnp.int32)
    for p in range(prompts):
        count = jnp.where(row == p, lengths[p], count)
    count = count.astype(jnp.float32)
    lines = turned.shape[0] // prompts
    features = jnp.concatenate(
        [turned[i * prompts : (i + 1) * prompts] / count for i in range(lines)], axis=1
    ).astype(jnp.bfloat16)
    width = valid.shape[0] // n_ranks
    for j in range(n_ranks):
        start = pl.multiple_of((j ^ me[0]) * width, width)
        level = lowest(j) if j else levels - 1
        at = j >> (level + 1) if j else 0
        outs[level][at] = dot_nt(features, valid[pl.ds(start, width), :])


def score(me, lengths, own, recv, valid, n_ranks):
    levels = n_ranks.bit_length()
    prompts = lengths.shape[0]
    width = valid.shape[0] // n_ranks
    counts = [n_ranks >> (b + 1) for b in range(levels - 1)] + [1]
    vmem = pl.BlockSpec(memory_space=pltpu.VMEM)
    smem = pl.BlockSpec(memory_space=pltpu.SMEM)
    return pl.pallas_call(
        functools.partial(score_kernel, n_ranks),
        in_specs=[smem, smem, vmem, vmem, vmem],
        out_specs=[vmem] * levels,
        out_shape=[jax.ShapeDtypeStruct((c, prompts, width), jnp.float32) for c in counts],
        name="score",
        cost_estimate=pl.CostEstimate(
            flops=2 * prompts * valid.size, bytes_accessed=2 * valid.size, transcendentals=0
        ),
        compiler_params=pltpu.CompilerParams(vmem_limit_bytes=VMEM_LIMIT),
    )(me, lengths, own, recv, valid)


def swap(value, axis, bit):
    count = lax.axis_size(axis)
    return lax.ppermute(value, axis, [(i, i ^ (1 << bit)) for i in range(count)])


def halving(groups, axis):
    for b in range(len(groups) - 1):
        got = swap(groups[b], axis, b)
        groups = list(groups)
        for c in range(b + 1, len(groups) - 1):
            step = 1 << (c - b)
            first = 1 << (c - b - 1)
            groups[c] = groups[c] + got[first::step]
        groups[-1] = groups[-1] + got[:1]
    return groups[-1]


def shards(inputs, out_grads, proj_in, proj_out, lengths, valid_feats):
    tok_rows = inputs.shape[0]
    n_ranks = lax.axis_size("tensor")
    top = n_ranks.bit_length() - 2
    n_blocks = n_ranks // 2
    me = jnp.stack([lax.axis_index("tensor"), lax.axis_index("dp")]).astype(jnp.int32)
    rank = proj_in.shape[1]
    size = tok_rows // n_blocks
    parts = [(0, size // 2), (size // 2, size // 2)]
    x, g, w_in, w_out = (
        pltpu.with_memory_space_constraint(v, pltpu.HBM)
        for v in (inputs, out_grads, proj_in.T, proj_out.T)
    )

    order = sorted(range(1, n_blocks), key=lambda j: (lowest(j), -j))
    pieces = [(j, c) for j in order for c in range(2)]
    if n_blocks == 4:
        pieces = [(3, 0), (3, 1), (1, 0), (2, 0), (1, 1), (2, 1)]
    pieces += [(0, 0), (0, 1)]
    spots = [(j, size, *parts[c]) for j, c in pieces]
    arrived, grams, held = {}, (), [w_in, w_out]
    for n, (j, c) in enumerate(pieces):
        depth = lowest(j) if j else top
        recvs = [arrived[(j | 1 << b, c)] for b in range(depth)]
        after = spots[n + 1] if n + 1 < len(spots) else None
        own, held = project(me, x, g, held, recvs if j else [], spots[n], after, n_blocks)
        if j:
            arrived[(j, c)] = swap(own, "tensor", depth)
        else:
            for r in recvs:
                own = own + r
            other = swap(own[: rank + rank // 2], "tensor", top)
            grams = gram(me, lengths, own, other, grams, spots[n], n_blocks, tok_rows)
    mine = halving(grams, "tensor")[0]
    dp_bits = lax.axis_size("dp").bit_length() - 1
    for b in range(dp_bits - 1):
        mine = mine + swap(mine, "dp", b)
    groups = score(me, lengths, mine, swap(mine, "dp", dp_bits - 1), valid_feats, n_ranks)
    return halving(groups, "tensor")[0]


def solution(mesh):
    return jax.shard_map(
        shards,
        mesh=mesh,
        in_specs=(
            P("dp", "tensor"),
            P("dp", "tensor"),
            P("tensor", None),
            P("tensor", None),
            P(),
            P("dp", "tensor"),
        ),
        out_specs=P(None, ("dp", "tensor")),
        check_vma=False,
    )
```

time: 211 us -> 85.7 us (0.41)
  waiting for transfers between devices: 158 us -> 31.7 us
  Pallas kernels: 0 us -> 33.9 us
  matrix products: 24.4 us -> 0 us
  starting transfers between devices: 0.04 us -> 18.9 us
  between operations: 13.5 us -> 0.17 us
  blocking collectives: 10.6 us -> 0 us
    psum x1 -> x0, waiting for transfers between devices: 104 us -> none  [shards(): summed_pair = lax.psum(paired, 'tensor')]
    reduce_scatter x1 -> x0, waiting for transfers between devices: 54 us -> none  [shards(): lax.psum_scatter(partial_value, 'tensor', scatter_dimension=1, tiled=True)]
    pallas_call x0 -> x11, Pallas kernels: none -> 33.9 us  [the longest x8 30.1 us: project(): pl.pallas_call(functools.partial(project_kernel, first, final, len(recvs)...]
    ppermute x0 -> x15, waiting for transfers between devices: none -> 31.7 us  [swap(): return lax.ppermute(value, axis, [(i, i ^ 1 << bit) for i in range(count)])]
    dot_general x4 -> x0, matrix products: 24.4 us -> none  [the longest x1 14.2 us: shards(): act_part = jnp.dot(inputs, proj_in, preferred_element_type=jnp.float32)]
    ppermute x0 -> x15, starting transfers between devices: none -> 18.9 us  [swap(): return lax.ppermute(value, axis, [(i, i ^ 1 << bit) for i in range(count)])]
    psum x1 -> x0, blocking collectives: 10.6 us -> none  [shards(): summed = lax.psum(gram_rows, 'dp')]
  transfers between devices with their start and end apart: 2 -> 15, of which waited for: 2 -> 9; matrix products, arithmetic and copies ran while one was open for 0% -> 0% of each run, Pallas kernels for 0% -> 31%
where the time goes in v1:
time: 85.7 us; the launch traced here: 85.6 us
  Pallas kernels  33.9 us (40%)
  waiting for transfers between devices  31.7 us (37%)
  starting transfers between devices  18.9 us (22%)
    ppermute x15, waiting for transfers between devices, swap(): return lax.ppermute(value, axis, [(i, i ^ 1 << bit) for i in range(count)])  31.7 us
    pallas_call x8, Pallas kernels, project(): pl.pallas_call(functools.partial(project_kernel, first, final, len(recvs)...  30.1 us
    ppermute x15, starting transfers between devices, swap(): return lax.ppermute(value, axis, [(i, i ^ 1 << bit) for i in range(count)])  18.9 us
    pallas_call x2, Pallas kernels, gram(): pl.pallas_call(functools.partial(gram_kernel, n_blocks, here, tok_rows, b...  2.7 us
  transfers between devices with their start and end apart: 15, of which 9 were waited for; matrix products, arithmetic and copies ran while one was open for 0% of the time, Pallas kernels for 31%

profile of v1, /device:TPU:0, one launch (start us, length us, event | category | flops | bytes accessed | tf_op | source)
XLA Modules:
  0.0 85.6 jit_solution(10665465882091524296)
XLA Ops:
  0.0 0.1 pad_add_fusion.me
  0.1 4.7 %project_3_0.1 = (f32[128,512]{1,0:T(8,128)S(1)}, bf16[512,3584]{1,0:T(8,128)(2,1)S(1)}, bf16[512,1024]{1,0:T(8,128)(2,1)S(1)}, bf16[64,3584]{1,0:T(8,128)(2,1)S(1)}, bf16[64,1024]{1,0:T(8,128)(2,1)S(1)}) custom-call(s32[2]{0:T(128)S(1)} %pad_add_fusion.me, bf16[4096,3584]{1,0:T(8,128)(2,1)} %x.15, bf16[4096,1024]{1,0:T(8,128)(2,1)} %g.15, ...), custom_call_target="tpu_custom_call" | custom-call | flops 603979776 | bytes 4718592 | tf_op jit(solution)/shard_map/project_3_0/pallas_call | solution.py:88
  4.8 3.0 %collective-permute-start = (f32[128,512]{1,0:T(8,128)S(1)}, f32[128,512]{1,0:T(8,128)S(1)}, u32[]{:S(2)}, u32[]{:S(2)}) collective-permute-start(f32[128,512]{1,0:T(8,128)S(1)} %get-tuple-element.46), channel_id=1, source_target_pairs={{0,1},{1,0},{2,3},{3,2},{4,5},{5,4},{6,7},{7,6},{8,9},{9,8},{10,11... | collective-permute-start | bytes 786440 | tf_op jit(solution)/shard_map/ppermute | solution.py:213
  7.8 4.0 %project_3_512.1 = (f32[128,512]{1,0:T(8,128)S(1)}, bf16[512,3584]{1,0:T(8,128)(2,1)S(1)}, bf16[512,1024]{1,0:T(8,128)(2,1)S(1)}) custom-call(s32[2]{0:T(128)S(1)} %pad_add_fusion.me, bf16[4096,3584]{1,0:T(8,128)(2,1)} %x.15, bf16[4096,1024]{1,0:T(8,128)(2,1)} %g.15, bf16[64,3584]{1,0:T(8,128)(2,1)S(1)} %get-tuple-element.38.refs_0_, ...), custom_call_target="tpu_custom_call" | custom-call | flops 603979776 | bytes 4718592 | tf_op jit(solution)/shard_map/project_3_512/pallas_call | solution.py:88
  11.8 0.1 collective-permute-start.1
  11.9 4.0 %project_1_0.1 = (f32[128,512]{1,0:T(8,128)S(1)}, bf16[512,3584]{1,0:T(8,128)(2,1)S(1)}, bf16[512,1024]{1,0:T(8,128)(2,1)S(1)}) custom-call(s32[2]{0:T(128)S(1)} %pad_add_fusion.me, bf16[4096,3584]{1,0:T(8,128)(2,1)} %x.15, bf16[4096,1024]{1,0:T(8,128)(2,1)} %g.15, bf16[64,3584]{1,0:T(8,128)(2,1)S(1)} %get-tuple-element.38.refs_0_, ...), custom_call_target="tpu_custom_call" | custom-call | flops 603979776 | bytes 4718592 | tf_op jit(solution)/shard_map/project_1_0/pallas_call | solution.py:88
  15.9 2.1 %collective-permute-start.5 = (f32[128,512]{1,0:T(8,128)S(1)}, f32[128,512]{1,0:T(8,128)S(1)}, u32[]{:S(2)}, u32[]{:S(2)}) collective-permute-start(f32[128,512]{1,0:T(8,128)S(1)} %get-tuple-element.59), channel_id=1, source_target_pairs={{0,1},{1,0},{2,3},{3,2},{4,5},{5,4},{6,7},{7,6},{8,9},{9,8},{10,11... | collective-permute-start | bytes 786440 | tf_op jit(solution)/shard_map/ppermute | solution.py:213
  18.0 0.0 collective-permute-done.refs_4_
  18.0 3.6 %project_2_0.1 = (f32[128,512]{1,0:T(8,128)S(1)}, bf16[512,3584]{1,0:T(8,128)(2,1)S(1)}, bf16[512,1024]{1,0:T(8,128)(2,1)S(1)}) custom-call(s32[2]{0:T(128)S(1)} %pad_add_fusion.me, bf16[4096,3584]{1,0:T(8,128)(2,1)} %x.15, bf16[4096,1024]{1,0:T(8,128)(2,1)} %g.15, bf16[64,3584]{1,0:T(8,128)(2,1)S(1)} %get-tuple-element.38.refs_0_, ...), custom_call_target="tpu_custom_call" | custom-call | flops 603979776 | bytes 4718592 | tf_op jit(solution)/shard_map/project_2_0/pallas_call | solution.py:88
  21.6 1.6 %collective-permute-start.6 = (f32[128,512]{1,0:T(8,128)S(1)}, f32[128,512]{1,0:T(8,128)S(1)}, u32[]{:S(2)}, u32[]{:S(2)}) collective-permute-start(f32[128,512]{1,0:T(8,128)S(1)} %get-tuple-element.60), channel_id=1, source_target_pairs={{0,2},{1,3},{2,0},{3,1},{4,6},{5,7},{6,4},{7,5},{8,10},{9,11},{10,... | collective-permute-start | bytes 786440 | tf_op jit(solution)/shard_map/ppermute | solution.py:213
  23.2 4.3 %project_1_512.1 = (f32[128,512]{1,0:T(8,128)S(1)}, bf16[512,3584]{1,0:T(8,128)(2,1)S(1)}, bf16[512,1024]{1,0:T(8,128)(2,1)S(1)}) custom-call(s32[2]{0:T(128)S(1)} %pad_add_fusion.me, bf16[4096,3584]{1,0:T(8,128)(2,1)} %x.15, bf16[4096,1024]{1,0:T(8,128)(2,1)} %g.15, bf16[64,3584]{1,0:T(8,128)(2,1)S(1)} %get-tuple-element.38.refs_0_, ...), custom_call_target="tpu_custom_call" | custom-call | flops 603979776 | bytes 4718592 | tf_op jit(solution)/shard_map/project_1_512/pallas_call | solution.py:88
  27.6 0.0 collective-permute-done.1.refs_4_
  27.6 3.4 %project_2_512.1 = (f32[128,512]{1,0:T(8,128)S(1)}, bf16[512,3584]{1,0:T(8,128)(2,1)S(1)}, bf16[512,1024]{1,0:T(8,128)(2,1)S(1)}) custom-call(s32[2]{0:T(128)S(1)} %pad_add_fusion.me, bf16[4096,3584]{1,0:T(8,128)(2,1)} %x.15, bf16[4096,1024]{1,0:T(8,128)(2,1)} %g.15, bf16[64,3584]{1,0:T(8,128)(2,1)S(1)} %get-tuple-element.38.refs_0_, ...), custom_call_target="tpu_custom_call" | custom-call | flops 603979776 | bytes 4718592 | tf_op jit(solution)/shard_map/project_2_512/pallas_call | solution.py:88
  31.0 0.5 collective-permute-start.3
  31.5 0.2 collective-permute-start.2
  31.6 4.0 %project_0_0.1 = (f32[128,512]{1,0:T(8,128)S(1)}, bf16[512,3584]{1,0:T(8,128)(2,1)S(1)}, bf16[512,1024]{1,0:T(8,128)(2,1)S(1)}) custom-call(s32[2]{0:T(128)S(1)} %pad_add_fusion.me, bf16[4096,3584]{1,0:T(8,128)(2,1)} %x.15, bf16[4096,1024]{1,0:T(8,128)(2,1)} %g.15, bf16[64,3584]{1,0:T(8,128)(2,1)S(1)} %get-tuple-element.38.refs_0_, ...), custom_call_target="tpu_custom_call" | custom-call | flops 603979776 | bytes 4718592 | tf_op jit(solution)/shard_map/project_0_0/pallas_call | solution.py:88
  35.7 0.0 copy-start.1
  35.7 2.1 %project_0_512.1 = f32[128,512]{1,0:T(8,128)S(1)} custom-call(s32[2]{0:T(128)S(1)} %pad_add_fusion.me, bf16[4096,3584]{1,0:T(8,128)(2,1)} %x.15, bf16[4096,1024]{1,0:T(8,128)(2,1)} %g.15, bf16[64,3584]{1,0:T(8,128)(2,1)S(1)} %get-tuple-element.38.refs_0_, bf16[64,1024]{1,0:T(8,128)(2,1)S(1)} %get-tuple-element.39.refs_1_, ...), custom_call_target="tpu_custom_call" | custom-call | flops 603979776 | bytes 4718592 | tf_op jit(solution)/shard_map/project_0_512/pallas_call | solution.py:88
  37.8 0.0 copy-start
  37.8 0.0 collective-permute-done.5
  37.8 0.0 collective-permute-done.6
  37.9 0.1 add_add_fusion.own
  37.9 3.0 %collective-permute-start.7 = (f32[96,512]{1,0:T(8,128)S(1)}, f32[96,512]{1,0:T(8,128)S(1)}, u32[]{:S(2)}, u32[]{:S(2)}) collective-permute-start(f32[96,512]{1,0:T(8,128)S(1)} %slice.40), channel_id=1, source_target_pairs={{0,4},{1,5},{2,6},{3,7},{4,0},{5,1},{6,2},{7,3},{8,12},{9,13},{10,... | collective-permute-start | bytes 589832 | tf_op jit(solution)/shard_map/ppermute | solution.py:213
  41.0 0.0 collective-permute-done.3
  41.0 0.0 collective-permute-done.2
  41.0 0.1 add_add_fusion.1.own
  41.1 0.1 collective-permute-start.4
  41.2 12.6 %collective-permute-done.7.recv = f32[96,512]{1,0:T(8,128)S(1)} collective-permute-done((f32[96,512]{1,0:T(8,128)S(1)}, f32[96,512]{1,0:T(8,128)S(1)}, u32[]{:S(2)}, u32[]{:S(2)}) %collective-permute-start.7) | collective-permute-done | bytes 196640 | tf_op jit(solution)/shard_map/ppermute | solution.py:213
  53.8 0.0 copy-done.1
  53.8 1.3 %gram_0.1 = (f32[2,64,128]{2,1,0:T(8,128)S(1)}, f32[1,64,128]{2,1,0:T(8,128)S(1)}, f32[1,64,128]{2,1,0:T(8,128)S(1)}) custom-call(s32[2]{0:T(128)S(1)} %pad_add_fusion.me, s32[16]{0:T(128)S(1)} %copy-done.1, f32[128,512]{1,0:T(8,128)S(1)} %add_add_fusion.own, f32[96,512]{1,0:T(8,128)S(1)} %collective-permute-done.7.recv), custom_call_target="tpu_custom_call" | custom-call | flops 100663296 | bytes 524288 | tf_op jit(solution)/shard_map/gram_0/pallas_call | solution.py:155
  55.1 1.8 %collective-permute-done.4.recv = f32[96,512]{1,0:T(8,128)S(1)} collective-permute-done((f32[96,512]{1,0:T(8,128)S(1)}, f32[96,512]{1,0:T(8,128)S(1)}, u32[]{:S(2)}, u32[]{:S(2)}) %collective-permute-start.4) | collective-permute-done | bytes 196640 | tf_op jit(solution)/shard_map/ppermute | solution.py:213
  56.8 1.4 %gram_512.1 = (f32[2,64,128]{2,1,0:T(8,128)S(1)}, f32[1,64,128]{2,1,0:T(8,128)S(1)}, f32[1,64,128]{2,1,0:T(8,128)S(1)}) custom-call(s32[2]{0:T(128)S(1)} %pad_add_fusion.me, s32[16]{0:T(128)S(1)} %copy-done.1, f32[128,512]{1,0:T(8,128)S(1)} %add_add_fusion.1.own, f32[96,512]{1,0:T(8,128)S(1)} %collective-permute-done.4.recv, ...), custom_call_target="tpu_custom_call" | custom-call | flops 100663296 | bytes 524288 | tf_op jit(solution)/shard_map/gram_512/pallas_call | solution.py:155
  58.2 1.6 %collective-permute-start.8 = (f32[2,64,128]{2,1,0:T(8,128)S(1)}, f32[2,64,128]{2,1,0:T(8,128)S(1)}, u32[]{:S(2)}, u32[]{:S(2)}) collective-permute-start(f32[2,64,128]{2,1,0:T(8,128)S(1)} %get-tuple-element.65), channel_id=1, source_target_pairs={{0,1},{1,0},{2,3},{3,2},{4,5},{5,4},{6,7},{7,6},{8,9},{9,8},{10,11... | collective-permute-start | bytes 196616 | tf_op jit(solution)/shard_map/ppermute | solution.py:213
  59.8 2.7 %collective-permute-done.8 = f32[2,64,128]{2,1,0:T(8,128)S(1)} collective-permute-done((f32[2,64,128]{2,1,0:T(8,128)S(1)}, f32[2,64,128]{2,1,0:T(8,128)S(1)}, u32[]{:S(2)}, u32[]{:S(2)}) %collective-permute-start.8) | collective-permute-done | bytes 65568 | tf_op jit(solution)/shard_map/ppermute | solution.py:213
  62.6 0.7 collective-permute-start.9
  63.3 3.2 %collective-permute-done.9 = f32[1,64,128]{2,1,0:T(8,128)S(1)} collective-permute-done((f32[1,64,128]{2,1,0:T(8,128)S(1)}, f32[1,64,128]{2,1,0:T(8,128)S(1)}, u32[]{:S(2)}, u32[]{:S(2)}) %collective-permute-start.9) | collective-permute-done | bytes 32800 | tf_op jit(solution)/shard_map/ppermute | solution.py:213
  66.5 0.1 collective-permute-start.10
  66.6 1.2 %collective-permute-done.10 = f32[64,128]{1,0:T(8,128)S(1)} collective-permute-done((f32[64,128]{1,0:T(8,128)S(1)}, f32[64,128]{1,0:T(8,128)S(1)}, u32[]{:S(2)}, u32[]{:S(2)}) %collective-permute-start.10) | collective-permute-done | bytes 32800 | tf_op jit(solution)/shard_map/ppermute | solution.py:213
  67.8 1.6 %collective-permute-start.11 = (f32[64,128]{1,0:T(8,128)S(1)}, f32[64,128]{1,0:T(8,128)S(1)}, u32[]{:S(2)}, u32[]{:S(2)}) collective-permute-start(f32[64,128]{1,0:T(8,128)S(1)} %add.49.own), channel_id=1, source_target_pairs={{0,16},{8,24},{16,0},{24,8},{1,17},{9,25},{17,1},{25,9},{2,18},{10... | collective-permute-start | bytes 98312 | tf_op jit(solution)/shard_map/ppermute | solution.py:213
  69.3 2.3 %collective-permute-done.11.recv = f32[64,128]{1,0:T(8,128)S(1)} collective-permute-done((f32[64,128]{1,0:T(8,128)S(1)}, f32[64,128]{1,0:T(8,128)S(1)}, u32[]{:S(2)}, u32[]{:S(2)}) %collective-permute-start.11) | collective-permute-done | bytes 32800 | tf_op jit(solution)/shard_map/ppermute | solution.py:213
  71.7 0.0 copy-done
  71.7 1.0 %score.1 = (f32[4,16,128]{2,1,0:T(8,128)S(1)}, f32[2,16,128]{2,1,0:T(8,128)S(1)}, f32[1,16,128]{2,1,0:T(8,128)S(1)}, f32[1,16,128]{2,1,0:T(8,128)S(1)}) custom-call(s32[2]{0:T(128)S(1)} %pad_add_fusion.me, s32[16]{0:T(128)S(1)} %copy-done.1, f32[64,128]{1,0:T(8,128)S(1)} %add.49.own, f32[64,128]{1,0:T(8,128)S(1)} %collective-permute-done.11.recv, ...), custom_call_target="tpu_custom_call" | custom-call | flops 16777216 | bytes 1048576 | tf_op jit(solution)/shard_map/score/pallas_call | solution.py:198
  72.7 1.6 %collective-permute-start.12 = (f32[4,16,128]{2,1,0:T(8,128)S(1)}, f32[4,16,128]{2,1,0:T(8,128)S(1)}, u32[]{:S(2)}, u32[]{:S(2)}) collective-permute-start(f32[4,16,128]{2,1,0:T(8,128)S(1)} %get-tuple-element.68), channel_id=1, source_target_pairs={{0,1},{1,0},{2,3},{3,2},{4,5},{5,4},{6,7},{7,6},{8,9},{9,8},{10,11... | collective-permute-start | bytes 98312 | tf_op jit(solution)/shard_map/ppermute | solution.py:213
  74.3 2.4 %collective-permute-done.12 = f32[4,16,128]{2,1,0:T(8,128)S(1)} collective-permute-done((f32[4,16,128]{2,1,0:T(8,128)S(1)}, f32[4,16,128]{2,1,0:T(8,128)S(1)}, u32[]{:S(2)}, u32[]{:S(2)}) %collective-permute-start.12) | collective-permute-done | bytes 32800 | tf_op jit(solution)/shard_map/ppermute | solution.py:213
  76.7 0.7 collective-permute-start.13
  77.4 3.0 %collective-permute-done.13 = f32[2,16,128]{2,1,0:T(8,128)S(1)} collective-permute-done((f32[2,16,128]{2,1,0:T(8,128)S(1)}, f32[2,16,128]{2,1,0:T(8,128)S(1)}, u32[]{:S(2)}, u32[]{:S(2)}) %collective-permute-start.13) | collective-permute-done | bytes 16416 | tf_op jit(solution)/shard_map/ppermute | solution.py:213
  80.4 2.1 %collective-permute-start.14 = (f32[1,16,128]{2,1,0:T(8,128)S(1)}, f32[1,16,128]{2,1,0:T(8,128)S(1)}, u32[]{:S(2)}, u32[]{:S(2)}) collective-permute-start(f32[1,16,128]{2,1,0:T(8,128)S(1)} %slice_add_fusion.3), channel_id=1, source_target_pairs={{0,4},{1,5},{2,6},{3,7},{4,0},{5,1},{6,2},{7,3},{8,12},{9,13},{10,... | collective-permute-start | bytes 24584 | tf_op jit(solution)/shard_map/ppermute | solution.py:213
  82.5 2.5 %collective-permute-done.14 = f32[1,16,128]{2,1,0:T(8,128)S(1)} collective-permute-done((f32[1,16,128]{2,1,0:T(8,128)S(1)}, f32[1,16,128]{2,1,0:T(8,128)S(1)}, u32[]{:S(2)}, u32[]{:S(2)}) %collective-permute-start.14) | collective-permute-done | bytes 8224 | tf_op jit(solution)/shard_map/ppermute | solution.py:213
  85.0 0.6 fusion.3
  (7 shorter events, 0.1 us)
Async XLA Ops:
  4.8 13.2 %collective-permute-start = (f32[128,512]{1,0:T(8,128)S(1)}, f32[128,512]{1,0:T(8,128)S(1)}, u32[]{:S(2)}, u32[]{:S(2)}) collective-permute-start(f32[128,512]{1,0:T(8,128)S(1)} %get-tuple-element.46), channel_id=1, source_target_pairs={{0,1},{1,0},{2,3},{3,2},{4,5},{5,4},{6,7},{7,6},{8,9},{9,8},{10,11... | collective-permute-start | bytes 786440 | tf_op jit(solution)/shard_map/ppermute | solution.py:213
  11.8 15.8 %collective-permute-start.1 = (f32[128,512]{1,0:T(8,128)S(1)}, f32[128,512]{1,0:T(8,128)S(1)}, u32[]{:S(2)}, u32[]{:S(2)}) collective-permute-start(f32[128,512]{1,0:T(8,128)S(1)} %get-tuple-element.51), channel_id=1, source_target_pairs={{0,1},{1,0},{2,3},{3,2},{4,5},{5,4},{6,7},{7,6},{8,9},{9,8},{10,11... | collective-permute-start | bytes 786440 | tf_op jit(solution)/shard_map/ppermute | solution.py:213
  15.9 21.9 %collective-permute-start.5 = (f32[128,512]{1,0:T(8,128)S(1)}, f32[128,512]{1,0:T(8,128)S(1)}, u32[]{:S(2)}, u32[]{:S(2)}) collective-permute-start(f32[128,512]{1,0:T(8,128)S(1)} %get-tuple-element.59), channel_id=1, source_target_pairs={{0,1},{1,0},{2,3},{3,2},{4,5},{5,4},{6,7},{7,6},{8,9},{9,8},{10,11... | collective-permute-start | bytes 786440 | tf_op jit(solution)/shard_map/ppermute | solution.py:213
  21.6 16.2 %collective-permute-start.6 = (f32[128,512]{1,0:T(8,128)S(1)}, f32[128,512]{1,0:T(8,128)S(1)}, u32[]{:S(2)}, u32[]{:S(2)}) collective-permute-start(f32[128,512]{1,0:T(8,128)S(1)} %get-tuple-element.60), channel_id=1, source_target_pairs={{0,2},{1,3},{2,0},{3,1},{4,6},{5,7},{6,4},{7,5},{8,10},{9,11},{10,... | collective-permute-start | bytes 786440 | tf_op jit(solution)/shard_map/ppermute | solution.py:213
  31.0 10.0 %collective-permute-start.3 = (f32[128,512]{1,0:T(8,128)S(1)}, f32[128,512]{1,0:T(8,128)S(1)}, u32[]{:S(2)}, u32[]{:S(2)}) collective-permute-start(f32[128,512]{1,0:T(8,128)S(1)} %get-tuple-element.57), channel_id=1, source_target_pairs={{0,2},{1,3},{2,0},{3,1},{4,6},{5,7},{6,4},{7,5},{8,10},{9,11},{10,... | collective-permute-start | bytes 786440 | tf_op jit(solution)/shard_map/ppermute | solution.py:213
  31.5 9.5 %collective-permute-start.2 = (f32[128,512]{1,0:T(8,128)S(1)}, f32[128,512]{1,0:T(8,128)S(1)}, u32[]{:S(2)}, u32[]{:S(2)}) collective-permute-start(f32[128,512]{1,0:T(8,128)S(1)} %get-tuple-element.56), channel_id=1, source_target_pairs={{0,1},{1,0},{2,3},{3,2},{4,5},{5,4},{6,7},{7,6},{8,9},{9,8},{10,11... | collective-permute-start | bytes 786440 | tf_op jit(solution)/shard_map/ppermute | solution.py:213
  35.7 18.1 %copy-start.1 = (s32[16]{0:T(128)S(1)}, s32[16]{0:T(128)}, u32[]{:S(2)}) copy-start(s32[16]{0:T(128)} %lengths.5) | copy-start | bytes 196
  37.8 33.9 %copy-start = (bf16[1024,512]{1,0:T(8,128)(2,1)S(1)}, bf16[1024,512]{1,0:T(8,128)(2,1)}, u32[]{:S(2)}) copy-start(bf16[1024,512]{1,0:T(8,128)(2,1)} %valid.1) | copy-start | bytes 3145732
  37.9 15.8 %collective-permute-start.7 = (f32[96,512]{1,0:T(8,128)S(1)}, f32[96,512]{1,0:T(8,128)S(1)}, u32[]{:S(2)}, u32[]{:S(2)}) collective-permute-start(f32[96,512]{1,0:T(8,128)S(1)} %slice.40), channel_id=1, source_target_pairs={{0,4},{1,5},{2,6},{3,7},{4,0},{5,1},{6,2},{7,3},{8,12},{9,13},{10,... | collective-permute-start | bytes 589832 | tf_op jit(solution)/shard_map/ppermute | solution.py:213
  41.1 15.8 %collective-permute-start.4 = (f32[96,512]{1,0:T(8,128)S(1)}, f32[96,512]{1,0:T(8,128)S(1)}, u32[]{:S(2)}, u32[]{:S(2)}) collective-permute-start(f32[96,512]{1,0:T(8,128)S(1)} %slice.39), channel_id=1, source_target_pairs={{0,4},{1,5},{2,6},{3,7},{4,0},{5,1},{6,2},{7,3},{8,12},{9,13},{10,... | collective-permute-start | bytes 589832 | tf_op jit(solution)/shard_map/ppermute | solution.py:213
  58.2 4.3 %collective-permute-start.8 = (f32[2,64,128]{2,1,0:T(8,128)S(1)}, f32[2,64,128]{2,1,0:T(8,128)S(1)}, u32[]{:S(2)}, u32[]{:S(2)}) collective-permute-start(f32[2,64,128]{2,1,0:T(8,128)S(1)} %get-tuple-element.65), channel_id=1, source_target_pairs={{0,1},{1,0},{2,3},{3,2},{4,5},{5,4},{6,7},{7,6},{8,9},{9,8},{10,11... | collective-permute-start | bytes 196616 | tf_op jit(solution)/shard_map/ppermute | solution.py:213
  62.6 3.9 %collective-permute-start.9 = (f32[1,64,128]{2,1,0:T(8,128)S(1)}, f32[1,64,128]{2,1,0:T(8,128)S(1)}, u32[]{:S(2)}, u32[]{:S(2)}) collective-permute-start(f32[1,64,128]{2,1,0:T(8,128)S(1)} %slice_add_fusion), channel_id=1, source_target_pairs={{0,2},{1,3},{2,0},{3,1},{4,6},{5,7},{6,4},{7,5},{8,10},{9,11},{10,... | collective-permute-start | bytes 98312 | tf_op jit(solution)/shard_map/ppermute | solution.py:213
  66.5 1.3 %collective-permute-start.10 = (f32[64,128]{1,0:T(8,128)S(1)}, f32[64,128]{1,0:T(8,128)S(1)}, u32[]{:S(2)}, u32[]{:S(2)}) collective-permute-start(f32[64,128]{1,0:T(8,128)S(1)} %fusion.1), channel_id=1, source_target_pairs={{0,8},{8,0},{16,24},{24,16},{1,9},{9,1},{17,25},{25,17},{2,10},{10... | collective-permute-start | bytes 98312 | tf_op jit(solution)/shard_map/ppermute | solution.py:213
  67.8 3.9 %collective-permute-start.11 = (f32[64,128]{1,0:T(8,128)S(1)}, f32[64,128]{1,0:T(8,128)S(1)}, u32[]{:S(2)}, u32[]{:S(2)}) collective-permute-start(f32[64,128]{1,0:T(8,128)S(1)} %add.49.own), channel_id=1, source_target_pairs={{0,16},{8,24},{16,0},{24,8},{1,17},{9,25},{17,1},{25,9},{2,18},{10... | collective-permute-start | bytes 98312 | tf_op jit(solution)/shard_map/ppermute | solution.py:213
  72.7 3.9 %collective-permute-start.12 = (f32[4,16,128]{2,1,0:T(8,128)S(1)}, f32[4,16,128]{2,1,0:T(8,128)S(1)}, u32[]{:S(2)}, u32[]{:S(2)}) collective-permute-start(f32[4,16,128]{2,1,0:T(8,128)S(1)} %get-tuple-element.68), channel_id=1, source_target_pairs={{0,1},{1,0},{2,3},{3,2},{4,5},{5,4},{6,7},{7,6},{8,9},{9,8},{10,11... | collective-permute-start | bytes 98312 | tf_op jit(solution)/shard_map/ppermute | solution.py:213
  76.7 3.7 %collective-permute-start.13 = (f32[2,16,128]{2,1,0:T(8,128)S(1)}, f32[2,16,128]{2,1,0:T(8,128)S(1)}, u32[]{:S(2)}, u32[]{:S(2)}) collective-permute-start(f32[2,16,128]{2,1,0:T(8,128)S(1)} %slice_add_fusion.2), channel_id=1, source_target_pairs={{0,2},{1,3},{2,0},{3,1},{4,6},{5,7},{6,4},{7,5},{8,10},{9,11},{10,... | collective-permute-start | bytes 49160 | tf_op jit(solution)/shard_map/ppermute | solution.py:213
  80.4 4.5 %collective-permute-start.14 = (f32[1,16,128]{2,1,0:T(8,128)S(1)}, f32[1,16,128]{2,1,0:T(8,128)S(1)}, u32[]{:S(2)}, u32[]{:S(2)}) collective-permute-start(f32[1,16,128]{2,1,0:T(8,128)S(1)} %slice_add_fusion.3), channel_id=1, source_target_pairs={{0,4},{1,5},{2,6},{3,7},{4,0},{5,1},{6,2},{7,3},{8,12},{9,13},{10,... | collective-permute-start | bytes 24584 | tf_op jit(solution)/shard_map/ppermute | solution.py:213

commit v2 on v1

--- a/solution.py
+++ b/solution.py
@@ -1,5 +1,4 @@
 import functools
-import math
 
 import jax
 import jax.numpy as jnp
@@ -8,8 +7,10 @@
 from jax.experimental.pallas import tpu as pltpu
 from jax.sharding import PartitionSpec as P
 
+
 NT = (((1,), (1,)), ((), ()))
 VMEM_LIMIT = 24 << 20
+AHEAD = 2
 
 
 def dot_nt(a, b):
@@ -20,85 +21,126 @@
     return (j & -j).bit_length() - 1
 
 
-def project_kernel(first, final, n_recv, n_blocks, here, after, me, x, g, *refs):
+def project_kernel(first, n_blocks, here, after, me, x, g, w_in, w_out, *refs):
     refs = list(refs)
-    ins = [refs.pop(0) for _ in range(2 if first else 4)]
-    recvs = [refs.pop(0) for _ in range(n_recv)]
-    out = refs.pop(0)
-    nexts = [] if final else [refs.pop(0), refs.pop(0)]
-    copies, sem = [], refs.pop()
-
-    def rows(at):
-        block, size, offset, count = at
-        start = (block ^ (me[0] & (n_blocks - 1))) * size + offset
-        return pl.ds(pl.multiple_of(start, math.gcd(size, offset, count)), count)
-
-    def fetch(source, target):
-        copy = pltpu.make_async_copy(source, target, sem.at[len(copies)])
-        copy.start()
-        copies.append(copy)
-
+    sent = (w_in, w_out)
+    if not first:
+        refs = refs[2:]
+    outs = [refs.pop(0) for _ in here]
+    ahead = (refs.pop(0), refs.pop(0)) if after else None
     if first:
-        w_in, w_out, x_now, g_now = refs
-        fetch(ins[0], w_in)
-        fetch(ins[1], w_out)
-        fetch(x.at[rows(here)], x_now)
-        fetch(g.at[rows(here)], g_now)
-    else:
-        w_in, w_out, x_now, g_now = ins
-    needed = len(copies)
-    if not final:
-        fetch(x.at[rows(after)], nexts[0])
-        fetch(g.at[rows(after)], nexts[1])
-    for copy in copies[:needed]:
-        copy.wait()
+        w_in, w_out = refs.pop(0), refs.pop(0)
+    x_rows, g_rows, sem, end_sem = refs
+    strip = x_rows.shape[1]
+
+    def rows(at, i):
+        block, size, offset, _ = at
+        start = (block ^ (me[0] & (n_blocks - 1))) * size + offset + i * strip
+        return pl.ds(pl.multiple_of(start, strip), strip)
+
+    late = []
+    if first:
+        for k in range(2):
+            late.append(pltpu.make_async_copy(sent[k], (w_in, w_out)[k], end_sem.at[k]))
+            late[-1].start()
+    places = strips_of(here, strip)
+    held = 0 if first else ahead_of(here, strip)
+    for slot in range(held, len(places)):
+        at, i = places[slot]
+        pltpu.make_async_copy(x.at[rows(at, i)], x_rows.at[slot], sem.at[slot, 0]).start()
+        pltpu.make_async_copy(g.at[rows(at, i)], g_rows.at[slot], sem.at[slot, 1]).start()
+    if after:
+        for slot in range(ahead_of(after, strip)):
+            at, i = strips_of(after, strip)[slot]
+            for k, source in enumerate((x, g)):
+                copy = pltpu.make_async_copy(
+                    source.at[rows(at, i)], ahead[k].at[slot], end_sem.at[2 + 2 * slot + k]
+                )
+                copy.start()
+                late.append(copy)
+    if first:
+        late.pop(0).wait()
+        late.pop(0).wait()
+
     rank = w_in.shape[0]
     half = rank // 2
     kept = me[0] // n_blocks
-    act = dot_nt(w_in[...], x_now[...])
-    grad = dot_nt(w_out[...], g_now[...])
-    total = jnp.zeros((2 * rank, act.shape[1]), jnp.float32)
-    for r in recvs:
-        total = total + r[...]
-    out[half : half + rank] = act if not recvs else act + total[half : half + rank]
-    for h in range(2):
-        to = pl.multiple_of(jnp.where(kept == h, half + rank, 0), half)
-        line = grad[h * half : (h + 1) * half]
-        for r in recvs:
-            line = line + r[pl.ds(to, half), :]
-        out[pl.ds(to, half), :] = line
-    for copy in copies[needed:]:
+    to = [pl.multiple_of(jnp.where(kept == h, half + rank, 0), half) for h in range(2)]
+
+    def body(slot, _):
+        @pl.when(slot >= held)
+        def _():
+            pltpu.make_async_copy(x_rows.at[slot], x_rows.at[slot], sem.at[slot, 0]).wait()
+            pltpu.make_async_copy(g_rows.at[slot], g_rows.at[slot], sem.at[slot, 1]).wait()
+
+        act = dot_nt(w_in[...], x_rows[slot])
+        grad = dot_nt(w_out[...], g_rows[slot])
+        begin = 0
+        for out, at in zip(outs, here):
+            end = begin + at[3] // strip
+
+            @pl.when((slot >= begin) & (slot < end))
+            def _(out=out, begin=begin):
+                cols = pl.ds(pl.multiple_of((slot - begin) * strip, strip), strip)
+                out[half : half + rank, cols] = act
+                for h in range(2):
+                    out[pl.ds(to[h], half), cols] = grad[h * half : (h + 1) * half]
+
+            begin = end
+        return 0
+
+    lax.fori_loop(0, len(places), body, 0)
+    for copy in late:
         copy.wait()
 
 
-def project(me, x, g, held, recvs, here, after, n_blocks):
-    first, final = len(held) == 2, after is None
+def strips_of(call, strip):
+    return [(at, i) for at in call for i in range(at[3] // strip)]
+
+
+def ahead_of(call, strip):
+    return min(AHEAD, len(strips_of(call, strip)))
+
+
+def project(me, x, g, held, here, after, n_blocks, strip):
+    first = len(held) == 2
     vmem = pl.BlockSpec(memory_space=pltpu.VMEM)
     hbm = pl.BlockSpec(memory_space=pltpu.HBM)
     smem = pl.BlockSpec(memory_space=pltpu.SMEM)
     rank = held[0].shape[0]
     wide = (x.shape[1], g.shape[1])
-    outs = [pltpu.VMEM((2 * rank, here[3]), jnp.float32)]
-    if not final:
-        outs += [pltpu.VMEM((after[3], w), jnp.bfloat16) for w in wide]
+    count = len(here)
+
+    def rows(call):
+        return [pltpu.VMEM((len(strips_of(call, strip)), strip, w), jnp.bfloat16) for w in wide]
+
+    outs = [pltpu.VMEM((2 * rank, at[3]), jnp.float32) for at in here]
+    if after:
+        outs += rows(after)
     if first:
         outs += [pltpu.VMEM(h.shape, h.dtype) for h in held]
-    scratch = [pltpu.VMEM((here[3], w), jnp.bfloat16) for w in wide] if first else []
-    size = here[3] * sum(wide)
+        scratch, aliases = rows(here), {}
+    else:
+        scratch, aliases = [], {5: len(outs), 6: len(outs) + 1}
+        outs += rows(here)
+    scratch += [
+        pltpu.SemaphoreType.DMA((len(strips_of(here, strip)), 2)),
+        pltpu.SemaphoreType.DMA((2 + 2 * AHEAD,)),
+    ]
+    size = sum(at[3] for at in here) * sum(wide)
     made = pl.pallas_call(
-        functools.partial(project_kernel, first, final, len(recvs), n_blocks, here, after),
-        in_specs=[smem, hbm, hbm] + [hbm if first else vmem] * len(held) + [vmem] * len(recvs),
+        functools.partial(project_kernel, first, n_blocks, here, after),
+        in_specs=[smem, hbm, hbm] + [hbm if first else vmem] * len(held),
         out_specs=[vmem] * len(outs),
         out_shape=outs,
-        scratch_shapes=scratch + [pltpu.SemaphoreType.DMA((6,))],
-        name=f"project_{here[0]}_{here[2]}",
+        scratch_shapes=scratch,
+        input_output_aliases=aliases,
         cost_estimate=pl.CostEstimate(flops=4 * rank * size, bytes_accessed=2 * size, transcendentals=0),
         compiler_params=pltpu.CompilerParams(vmem_limit_bytes=VMEM_LIMIT),
-    )(me, x, g, *held, *recvs)
+    )(me, x, g, *held)
     made = list(made)
-    if first:
-        return made[0], [made[3], made[4], made[1], made[2]]
-    return made[0], list(held[:2]) + made[1:]
+    weights = made[count + 2 : count + 4] if first else list(held[:2])
+    return made[:count], weights + made[count : count + 2]
 
 
 def gram_kernel(n_blocks, here, tok_rows, has_prev, me, lengths, own, recv, *refs):
@@ -158,7 +200,6 @@
         out_specs=[vmem] * levels,
         out_shape=[jax.ShapeDtypeStruct((c, 2 * half, width), jnp.float32) for c in counts],
         scratch_shapes=[pltpu.VMEM((half * prompts, piece), jnp.bfloat16)] * 2,
-        name=f"gram_{here[2]}",
         cost_estimate=pl.CostEstimate(
             flops=12 * half * half * prompts * piece, bytes_accessed=8 * own.size, transcendentals=0
         ),
@@ -225,6 +266,13 @@
     return groups[-1]
 
 
+def plan(n_blocks):
+    if n_blocks == 4:
+        return [[(3, 0)], [(3, 1), (1, 0), (2, 0)], [(2, 1), (1, 1), (0, 0)], [(0, 1)]]
+    order = sorted(range(1, n_blocks), key=lambda j: (lowest(j), -j))
+    return [[(j, 0), (j, 1)] for j in order] + [[(0, 0), (0, 1)]]
+
+
 def shards(inputs, out_grads, proj_in, proj_out, lengths, valid_feats):
     tok_rows = inputs.shape[0]
     n_ranks = lax.axis_size("tensor")
@@ -234,30 +282,27 @@
     rank = proj_in.shape[1]
     size = tok_rows // n_blocks
     parts = [(0, size // 2), (size // 2, size // 2)]
+    strip = min(256, size // 2)
     x, g, w_in, w_out = (
         pltpu.with_memory_space_constraint(v, pltpu.HBM)
         for v in (inputs, out_grads, proj_in.T, proj_out.T)
     )
 
-    order = sorted(range(1, n_blocks), key=lambda j: (lowest(j), -j))
-    pieces = [(j, c) for j in order for c in range(2)]
-    if n_blocks == 4:
-        pieces = [(3, 0), (3, 1), (1, 0), (2, 0), (1, 1), (2, 1)]
-    pieces += [(0, 0), (0, 1)]
-    spots = [(j, size, *parts[c]) for j, c in pieces]
+    calls = plan(n_blocks)
+    spots = [[(j, size, *parts[c]) for j, c in call] for call in calls]
     arrived, grams, held = {}, (), [w_in, w_out]
-    for n, (j, c) in enumerate(pieces):
-        depth = lowest(j) if j else top
-        recvs = [arrived[(j | 1 << b, c)] for b in range(depth)]
+    for n, call in enumerate(calls):
         after = spots[n + 1] if n + 1 < len(spots) else None
-        own, held = project(me, x, g, held, recvs if j else [], spots[n], after, n_blocks)
-        if j:
-            arrived[(j, c)] = swap(own, "tensor", depth)
-        else:
-            for r in recvs:
-                own = own + r
-            other = swap(own[: rank + rank // 2], "tensor", top)
-            grams = gram(me, lengths, own, other, grams, spots[n], n_blocks, tok_rows)
+        made, held = project(me, x, g, held, spots[n], after, n_blocks, strip)
+        for (j, c), own, spot in zip(call, made, spots[n]):
+            depth = lowest(j) if j else top
+            for b in range(depth):
+                own = own + arrived[(j | 1 << b, c)]
+            if j:
+                arrived[(j, c)] = swap(own, "tensor", depth)
+            else:
+                other = swap(own[: rank + rank // 2], "tensor", top)
+                grams = gram(me, lengths, own, other, grams, spot, n_blocks, tok_rows)
     mine = halving(grams, "tensor")[0]
     dp_bits = lax.axis_size("dp").bit_length() - 1
     for b in range(dp_bits - 1):
@@ -267,17 +312,21 @@
 
 
 def solution(mesh):
-    return jax.shard_map(
-        shards,
-        mesh=mesh,
-        in_specs=(
-            P("dp", "tensor"),
-            P("dp", "tensor"),
-            P("tensor", None),
-            P("tensor", None),
-            P(),
-            P("dp", "tensor"),
-        ),
-        out_specs=P(None, ("dp", "tensor")),
-        check_vma=False,
-    )
+    def program(inputs, *rest):
+        run = jax.shard_map(
+            shards,
+            mesh=mesh,
+            in_specs=(
+                P("dp", "tensor"),
+                P("dp", "tensor"),
+                P("tensor", None),
+                P("tensor", None),
+                P(),
+                P("dp", "tensor"),
+            ),
+            out_specs=P(None, ("dp", "tensor")),
+            check_vma=False,
+        )
+        return run(inputs, *rest)
+
+    return program

time: 85.7 us -> 76.6 us (0.89)
  Pallas kernels: 33.9 us -> 24.1 us
    pallas_call x8 -> x4, Pallas kernels: 30.1 us -> 20.4 us  [project(): pl.pallas_call(functools.partial(project_kernel, first, n_blocks, here, a...]
  transfers between devices with their start and end apart: 15 -> 15, of which waited for: 9 -> 12; matrix products, arithmetic and copies ran while one was open for 0% -> 0% of each run, Pallas kernels for 31% -> 22%
where the time goes in v2:
time: 76.6 us; the launch traced here: 76.5 us
  waiting for transfers between devices  32.2 us (42%)
  Pallas kernels  24.1 us (31%)
  starting transfers between devices  19.2 us (25%)
  other arithmetic  0.89 us (1%)
    ppermute x15, waiting for transfers between devices, swap(): return lax.ppermute(value, axis, [(i, i ^ 1 << bit) for i in range(count)])  32.2 us
    pallas_call x4, Pallas kernels, project(): pl.pallas_call(functools.partial(project_kernel, first, n_blocks, here, a...  20.4 us
    ppermute x15, starting transfers between devices, swap(): return lax.ppermute(value, axis, [(i, i ^ 1 << bit) for i in range(count)])  19.2 us
    pallas_call x2, Pallas kernels, gram(): pl.pallas_call(functools.partial(gram_kernel, n_blocks, here, tok_rows, b...  2.7 us
  transfers between devices with their start and end apart: 15, of which 12 were waited for; matrix products, arithmetic and copies ran while one was open for 0% of the time, Pallas kernels for 22%

profile of v2, /device:TPU:0, one launch (start us, length us, event | category | flops | bytes accessed | tf_op | source)
XLA Modules:
  0.0 76.5 jit_solution(8851510627917508983)
XLA Ops:
  0.0 0.1 pad_add_fusion.me
  0.1 5.2 %shard_map.64 = (f32[128,512]{1,0:T(8,128)S(1)}, bf16[6,256,3584]{2,1,0:T(8,128)(2,1)S(1)}, bf16[6,256,1024]{2,1,0:T(8,128)(2,1)S(1)}, bf16[64,3584]{1,0:T(8,128)(2,1)S(1)}, bf16[64,1024]{1,0:T(8,128)(2,1)S(1)}) custom-call(s32[2]{0:T(128)S(1)} %pad_add_fusion.me, bf16[4096,3584]{1,0:T(8,128)(2,1)} %x.7, bf16[4096,1024]{1,0:T(8,128)(2,1)} %g.7, ...), custom_call_target="tpu_custom_call" | custom-call | flops 603979776 | bytes 4718592 | tf_op jit(solution)/shard_map/pallas_call | solution.py:131
  5.3 3.0 %collective-permute-start.5 = (f32[128,512]{1,0:T(8,128)S(1)}, f32[128,512]{1,0:T(8,128)S(1)}, u32[]{:S(2)}, u32[]{:S(2)}) collective-permute-start(f32[128,512]{1,0:T(8,128)S(1)} %get-tuple-element.46), channel_id=1, source_target_pairs={{0,1},{1,0},{2,3},{3,2},{4,5},{5,4},{6,7},{7,6},{8,9},{9,8},{10,11... | collective-permute-start | bytes 786440 | tf_op jit(solution)/shard_map/ppermute | solution.py:254
  8.3 6.5 %shard_map.65 = (f32[128,512]{1,0:T(8,128)S(1)}, f32[128,512]{1,0:T(8,128)S(1)}, f32[128,512]{1,0:T(8,128)S(1)}, bf16[6,256,3584]{2,1,0:T(8,128)(2,1)S(1)}, bf16...) custom-call(s32[2]{0:T(128)S(1)} %pad_add_fusion.me, ...), custom_call_target="tpu_custom_call", output_to_operand_aliasing={{5}: (5, {}), {6}: (6, {})} | custom-call | flops 1811939328 | bytes 14155776 | tf_op jit(solution)/shard_map/pallas_call | solution.py:131
  14.8 0.1 collective-permute-start.1
  14.9 2.0 %collective-permute-start.4 = (f32[128,512]{1,0:T(8,128)S(1)}, f32[128,512]{1,0:T(8,128)S(1)}, u32[]{:S(2)}, u32[]{:S(2)}) collective-permute-start(f32[128,512]{1,0:T(8,128)S(1)} %get-tuple-element.44), channel_id=1, source_target_pairs={{0,1},{1,0},{2,3},{3,2},{4,5},{5,4},{6,7},{7,6},{8,9},{9,8},{10,11... | collective-permute-start | bytes 786440 | tf_op jit(solution)/shard_map/ppermute | solution.py:254
  16.9 0.0 collective-permute-done.5
  16.9 1.7 %collective-permute-start.6 = (f32[128,512]{1,0:T(8,128)S(1)}, f32[128,512]{1,0:T(8,128)S(1)}, u32[]{:S(2)}, u32[]{:S(2)}) collective-permute-start(f32[128,512]{1,0:T(8,128)S(1)} %add.52), channel_id=1, source_target_pairs={{0,2},{1,3},{2,0},{3,1},{4,6},{5,7},{6,4},{7,5},{8,10},{9,11},{10,... | collective-permute-start | bytes 786440 | tf_op jit(solution)/shard_map/ppermute | solution.py:254
  18.7 6.4 %shard_map.66 = (f32[128,512]{1,0:T(8,128)S(1)}, f32[128,512]{1,0:T(8,128)S(1)}, f32[128,512]{1,0:T(8,128)S(1)}, bf16[2,256,3584]{2,1,0:T(8,128)(2,1)S(1)}, bf16...) custom-call(s32[2]{0:T(128)S(1)} %pad_add_fusion.me, ...), custom_call_target="tpu_custom_call", output_to_operand_aliasing={{5}: (5, {}), {6}: (6, {})} | custom-call | flops 1811939328 | bytes 14155776 | tf_op jit(solution)/shard_map/pallas_call | solution.py:131
  25.1 0.5 collective-permute-start
  25.5 0.0 collective-permute-done.1
  25.6 0.2 collective-permute-start.2
  25.8 0.0 copy-start.1
  25.8 0.0 copy-start
  25.8 2.3 %shard_map.67 = (f32[128,512]{1,0:T(8,128)S(1)}, bf16[2,256,3584]{2,1,0:T(8,128)(2,1)S(1)}, bf16[2,256,1024]{2,1,0:T(8,128)(2,1)S(1)}) custom-call(s32[2]{0:T(128)S(1)} %pad_add_fusion.me, bf16[4096,3584]{1,0:T(8,128)(2,1)} %x.7, bf16[4096,1024]{1,0:T(8,128)(2,1)} %g.7, ...), custom_call_target="tpu_custom_call", output_to_operand_aliasing={{1}: (5, {}), {2}: (6, {})} | custom-call | flops 603979776 | bytes 4718592 | tf_op jit(solution)/shard_map/pallas_call | solution.py:131
  28.1 1.5 %collective-permute-done.4 = f32[128,512]{1,0:T(8,128)S(1)} collective-permute-done((f32[128,512]{1,0:T(8,128)S(1)}, f32[128,512]{1,0:T(8,128)S(1)}, u32[]{:S(2)}, u32[]{:S(2)}) %collective-permute-start.4) | collective-permute-done | bytes 262176 | tf_op jit(solution)/shard_map/ppermute | solution.py:254
  29.6 0.0 collective-permute-done.6
  29.6 0.1 add_add_fusion.own
  29.7 2.7 %collective-permute-start.7 = (f32[96,512]{1,0:T(8,128)S(1)}, f32[96,512]{1,0:T(8,128)S(1)}, u32[]{:S(2)}, u32[]{:S(2)}) collective-permute-start(f32[96,512]{1,0:T(8,128)S(1)} %slice.40), channel_id=1, source_target_pairs={{0,4},{1,5},{2,6},{3,7},{4,0},{5,1},{6,2},{7,3},{8,12},{9,13},{10,... | collective-permute-start | bytes 589832 | tf_op jit(solution)/shard_map/ppermute | solution.py:254
  32.4 1.5 %collective-permute-done = f32[128,512]{1,0:T(8,128)S(1)} collective-permute-done((f32[128,512]{1,0:T(8,128)S(1)}, f32[128,512]{1,0:T(8,128)S(1)}, u32[]{:S(2)}, u32[]{:S(2)}) %collective-permute-start) | collective-permute-done | bytes 262176 | tf_op jit(solution)/shard_map/ppermute | solution.py:254
  33.8 0.7 collective-permute-done.2
  34.5 0.1 add_add_fusion.1.own
  34.6 2.5 %collective-permute-start.3 = (f32[96,512]{1,0:T(8,128)S(1)}, f32[96,512]{1,0:T(8,128)S(1)}, u32[]{:S(2)}, u32[]{:S(2)}) collective-permute-start(f32[96,512]{1,0:T(8,128)S(1)} %slice.39), channel_id=1, source_target_pairs={{0,4},{1,5},{2,6},{3,7},{4,0},{5,1},{6,2},{7,3},{8,12},{9,13},{10,... | collective-permute-start | bytes 589832 | tf_op jit(solution)/shard_map/ppermute | solution.py:254
  37.1 7.5 %collective-permute-done.7.recv = f32[96,512]{1,0:T(8,128)S(1)} collective-permute-done((f32[96,512]{1,0:T(8,128)S(1)}, f32[96,512]{1,0:T(8,128)S(1)}, u32[]{:S(2)}, u32[]{:S(2)}) %collective-permute-start.7) | collective-permute-done | bytes 196640 | tf_op jit(solution)/shard_map/ppermute | solution.py:254
  44.6 0.0 copy-done.1
  44.6 1.3 %shard_map.68 = (f32[2,64,128]{2,1,0:T(8,128)S(1)}, f32[1,64,128]{2,1,0:T(8,128)S(1)}, f32[1,64,128]{2,1,0:T(8,128)S(1)}) custom-call(s32[2]{0:T(128)S(1)} %pad_add_fusion.me, s32[16]{0:T(128)S(1)} %copy-done.1, f32[128,512]{1,0:T(8,128)S(1)} %add_add_fusion.own, f32[96,512]{1,0:T(8,128)S(1)} %collective-permute-done.7.recv), custom_call_target="tpu_custom_call" | custom-call | flops 100663296 | bytes 524288 | tf_op jit(solution)/shard_map/pallas_call | solution.py:197
  45.9 1.9 %collective-permute-done.3.recv = f32[96,512]{1,0:T(8,128)S(1)} collective-permute-done((f32[96,512]{1,0:T(8,128)S(1)}, f32[96,512]{1,0:T(8,128)S(1)}, u32[]{:S(2)}, u32[]{:S(2)}) %collective-permute-start.3) | collective-permute-done | bytes 196640 | tf_op jit(solution)/shard_map/ppermute | solution.py:254
  47.8 1.4 %shard_map.69 = (f32[2,64,128]{2,1,0:T(8,128)S(1)}, f32[1,64,128]{2,1,0:T(8,128)S(1)}, f32[1,64,128]{2,1,0:T(8,128)S(1)}) custom-call(s32[2]{0:T(128)S(1)} %pad_add_fusion.me, s32[16]{0:T(128)S(1)} %copy-done.1, f32[128,512]{1,0:T(8,128)S(1)} %add_add_fusion.1.own, f32[96,512]{1,0:T(8,128)S(1)} %collective-permute-done.3.recv, ...), custom_call_target="tpu_custom_call" | custom-call | flops 100663296 | bytes 524288 | tf_op jit(solution)/shard_map/pallas_call | solution.py:197
  49.2 1.1 %collective-permute-start.8 = (f32[2,64,128]{2,1,0:T(8,128)S(1)}, f32[2,64,128]{2,1,0:T(8,128)S(1)}, u32[]{:S(2)}, u32[]{:S(2)}) collective-permute-start(f32[2,64,128]{2,1,0:T(8,128)S(1)} %get-tuple-element.51), channel_id=1, source_target_pairs={{0,1},{1,0},{2,3},{3,2},{4,5},{5,4},{6,7},{7,6},{8,9},{9,8},{10,11... | collective-permute-start | bytes 196616 | tf_op jit(solution)/shard_map/ppermute | solution.py:254
  50.3 3.2 %collective-permute-done.8 = f32[2,64,128]{2,1,0:T(8,128)S(1)} collective-permute-done((f32[2,64,128]{2,1,0:T(8,128)S(1)}, f32[2,64,128]{2,1,0:T(8,128)S(1)}, u32[]{:S(2)}, u32[]{:S(2)}) %collective-permute-start.8) | collective-permute-done | bytes 65568 | tf_op jit(solution)/shard_map/ppermute | solution.py:254
  53.5 0.4 collective-permute-start.9
  54.0 3.5 %collective-permute-done.9 = f32[1,64,128]{2,1,0:T(8,128)S(1)} collective-permute-done((f32[1,64,128]{2,1,0:T(8,128)S(1)}, f32[1,64,128]{2,1,0:T(8,128)S(1)}, u32[]{:S(2)}, u32[]{:S(2)}) %collective-permute-start.9) | collective-permute-done | bytes 32800 | tf_op jit(solution)/shard_map/ppermute | solution.py:254
  57.4 0.1 collective-permute-start.10
  57.5 1.2 %collective-permute-done.10 = f32[64,128]{1,0:T(8,128)S(1)} collective-permute-done((f32[64,128]{1,0:T(8,128)S(1)}, f32[64,128]{1,0:T(8,128)S(1)}, u32[]{:S(2)}, u32[]{:S(2)}) %collective-permute-start.10) | collective-permute-done | bytes 32800 | tf_op jit(solution)/shard_map/ppermute | solution.py:254
  58.7 1.5 %collective-permute-start.11 = (f32[64,128]{1,0:T(8,128)S(1)}, f32[64,128]{1,0:T(8,128)S(1)}, u32[]{:S(2)}, u32[]{:S(2)}) collective-permute-start(f32[64,128]{1,0:T(8,128)S(1)} %add.57.own), channel_id=1, source_target_pairs={{0,16},{8,24},{16,0},{24,8},{1,17},{9,25},{17,1},{25,9},{2,18},{10... | collective-permute-start | bytes 98312 | tf_op jit(solution)/shard_map/ppermute | solution.py:254
  60.2 2.4 %collective-permute-done.11.recv = f32[64,128]{1,0:T(8,128)S(1)} collective-permute-done((f32[64,128]{1,0:T(8,128)S(1)}, f32[64,128]{1,0:T(8,128)S(1)}, u32[]{:S(2)}, u32[]{:S(2)}) %collective-permute-start.11) | collective-permute-done | bytes 32800 | tf_op jit(solution)/shard_map/ppermute | solution.py:254
  62.6 0.0 copy-done
  62.6 1.0 %score.1 = (f32[4,16,128]{2,1,0:T(8,128)S(1)}, f32[2,16,128]{2,1,0:T(8,128)S(1)}, f32[1,16,128]{2,1,0:T(8,128)S(1)}, f32[1,16,128]{2,1,0:T(8,128)S(1)}) custom-call(s32[2]{0:T(128)S(1)} %pad_add_fusion.me, s32[16]{0:T(128)S(1)} %copy-done.1, f32[64,128]{1,0:T(8,128)S(1)} %add.57.own, f32[64,128]{1,0:T(8,128)S(1)} %collective-permute-done.11.recv, ...), custom_call_target="tpu_custom_call" | custom-call | flops 16777216 | bytes 1048576 | tf_op jit(solution)/shard_map/score/pallas_call | solution.py:239
  63.7 1.1 %collective-permute-start.12 = (f32[4,16,128]{2,1,0:T(8,128)S(1)}, f32[4,16,128]{2,1,0:T(8,128)S(1)}, u32[]{:S(2)}, u32[]{:S(2)}) collective-permute-start(f32[4,16,128]{2,1,0:T(8,128)S(1)} %get-tuple-element.54), channel_id=1, source_target_pairs={{0,1},{1,0},{2,3},{3,2},{4,5},{5,4},{6,7},{7,6},{8,9},{9,8},{10,11... | collective-permute-start | bytes 98312 | tf_op jit(solution)/shard_map/ppermute | solution.py:254
  64.7 2.9 %collective-permute-done.12 = f32[4,16,128]{2,1,0:T(8,128)S(1)} collective-permute-done((f32[4,16,128]{2,1,0:T(8,128)S(1)}, f32[4,16,128]{2,1,0:T(8,128)S(1)}, u32[]{:S(2)}, u32[]{:S(2)}) %collective-permute-start.12) | collective-permute-done | bytes 32800 | tf_op jit(solution)/shard_map/ppermute | solution.py:254
  67.6 0.4 collective-permute-start.13
  68.0 3.3 %collective-permute-done.13 = f32[2,16,128]{2,1,0:T(8,128)S(1)} collective-permute-done((f32[2,16,128]{2,1,0:T(8,128)S(1)}, f32[2,16,128]{2,1,0:T(8,128)S(1)}, u32[]{:S(2)}, u32[]{:S(2)}) %collective-permute-start.13) | collective-permute-done | bytes 16416 | tf_op jit(solution)/shard_map/ppermute | solution.py:254
  71.3 1.8 %collective-permute-start.14 = (f32[1,16,128]{2,1,0:T(8,128)S(1)}, f32[1,16,128]{2,1,0:T(8,128)S(1)}, u32[]{:S(2)}, u32[]{:S(2)}) collective-permute-start(f32[1,16,128]{2,1,0:T(8,128)S(1)} %slice_add_fusion.3), channel_id=1, source_target_pairs={{0,4},{1,5},{2,6},{3,7},{4,0},{5,1},{6,2},{7,3},{8,12},{9,13},{10,... | collective-permute-start | bytes 24584 | tf_op jit(solution)/shard_map/ppermute | solution.py:254
  73.1 2.7 %collective-permute-done.14 = f32[1,16,128]{2,1,0:T(8,128)S(1)} collective-permute-done((f32[1,16,128]{2,1,0:T(8,128)S(1)}, f32[1,16,128]{2,1,0:T(8,128)S(1)}, u32[]{:S(2)}, u32[]{:S(2)}) %collective-permute-start.14) | collective-permute-done | bytes 8224 | tf_op jit(solution)/shard_map/ppermute | solution.py:254
  75.9 0.6 fusion.3
  (9 shorter events, 0.1 us)
Async XLA Ops:
  5.3 11.6 %collective-permute-start.5 = (f32[128,512]{1,0:T(8,128)S(1)}, f32[128,512]{1,0:T(8,128)S(1)}, u32[]{:S(2)}, u32[]{:S(2)}) collective-permute-start(f32[128,512]{1,0:T(8,128)S(1)} %get-tuple-element.46), channel_id=1, source_target_pairs={{0,1},{1,0},{2,3},{3,2},{4,5},{5,4},{6,7},{7,6},{8,9},{9,8},{10,11... | collective-permute-start | bytes 786440 | tf_op jit(solution)/shard_map/ppermute | solution.py:254
  14.8 10.7 %collective-permute-start.1 = (f32[128,512]{1,0:T(8,128)S(1)}, f32[128,512]{1,0:T(8,128)S(1)}, u32[]{:S(2)}, u32[]{:S(2)}) collective-permute-start(f32[128,512]{1,0:T(8,128)S(1)} %get-tuple-element.42), channel_id=1, source_target_pairs={{0,1},{1,0},{2,3},{3,2},{4,5},{5,4},{6,7},{7,6},{8,9},{9,8},{10,11... | collective-permute-start | bytes 786440 | tf_op jit(solution)/shard_map/ppermute | solution.py:254
  14.9 14.8 %collective-permute-start.4 = (f32[128,512]{1,0:T(8,128)S(1)}, f32[128,512]{1,0:T(8,128)S(1)}, u32[]{:S(2)}, u32[]{:S(2)}) collective-permute-start(f32[128,512]{1,0:T(8,128)S(1)} %get-tuple-element.44), channel_id=1, source_target_pairs={{0,1},{1,0},{2,3},{3,2},{4,5},{5,4},{6,7},{7,6},{8,9},{9,8},{10,11... | collective-permute-start | bytes 786440 | tf_op jit(solution)/shard_map/ppermute | solution.py:254
  16.9 12.7 %collective-permute-start.6 = (f32[128,512]{1,0:T(8,128)S(1)}, f32[128,512]{1,0:T(8,128)S(1)}, u32[]{:S(2)}, u32[]{:S(2)}) collective-permute-start(f32[128,512]{1,0:T(8,128)S(1)} %add.52), channel_id=1, source_target_pairs={{0,2},{1,3},{2,0},{3,1},{4,6},{5,7},{6,4},{7,5},{8,10},{9,11},{10,... | collective-permute-start | bytes 786440 | tf_op jit(solution)/shard_map/ppermute | solution.py:254
  25.1 8.8 %collective-permute-start = (f32[128,512]{1,0:T(8,128)S(1)}, f32[128,512]{1,0:T(8,128)S(1)}, u32[]{:S(2)}, u32[]{:S(2)}) collective-permute-start(f32[128,512]{1,0:T(8,128)S(1)} %get-tuple-element.40), channel_id=1, source_target_pairs={{0,1},{1,0},{2,3},{3,2},{4,5},{5,4},{6,7},{7,6},{8,9},{9,8},{10,11... | collective-permute-start | bytes 786440 | tf_op jit(solution)/shard_map/ppermute | solution.py:254
  25.6 8.9 %collective-permute-start.2 = (f32[128,512]{1,0:T(8,128)S(1)}, f32[128,512]{1,0:T(8,128)S(1)}, u32[]{:S(2)}, u32[]{:S(2)}) collective-permute-start(f32[128,512]{1,0:T(8,128)S(1)} %add.49), channel_id=1, source_target_pairs={{0,2},{1,3},{2,0},{3,1},{4,6},{5,7},{6,4},{7,5},{8,10},{9,11},{10,... | collective-permute-start | bytes 786440 | tf_op jit(solution)/shard_map/ppermute | solution.py:254
  25.8 18.8 %copy-start.1 = (s32[16]{0:T(128)S(1)}, s32[16]{0:T(128)}, u32[]{:S(2)}) copy-start(s32[16]{0:T(128)} %lengths.5) | copy-start | bytes 196
  25.8 36.8 %copy-start = (bf16[1024,512]{1,0:T(8,128)(2,1)S(1)}, bf16[1024,512]{1,0:T(8,128)(2,1)}, u32[]{:S(2)}) copy-start(bf16[1024,512]{1,0:T(8,128)(2,1)} %valid.1) | copy-start | bytes 3145732
  29.7 14.9 %collective-permute-start.7 = (f32[96,512]{1,0:T(8,128)S(1)}, f32[96,512]{1,0:T(8,128)S(1)}, u32[]{:S(2)}, u32[]{:S(2)}) collective-permute-start(f32[96,512]{1,0:T(8,128)S(1)} %slice.40), channel_id=1, source_target_pairs={{0,4},{1,5},{2,6},{3,7},{4,0},{5,1},{6,2},{7,3},{8,12},{9,13},{10,... | collective-permute-start | bytes 589832 | tf_op jit(solution)/shard_map/ppermute | solution.py:254
  34.6 13.2 %collective-permute-start.3 = (f32[96,512]{1,0:T(8,128)S(1)}, f32[96,512]{1,0:T(8,128)S(1)}, u32[]{:S(2)}, u32[]{:S(2)}) collective-permute-start(f32[96,512]{1,0:T(8,128)S(1)} %slice.39), channel_id=1, source_target_pairs={{0,4},{1,5},{2,6},{3,7},{4,0},{5,1},{6,2},{7,3},{8,12},{9,13},{10,... | collective-permute-start | bytes 589832 | tf_op jit(solution)/shard_map/ppermute | solution.py:254
  49.2 4.3 %collective-permute-start.8 = (f32[2,64,128]{2,1,0:T(8,128)S(1)}, f32[2,64,128]{2,1,0:T(8,128)S(1)}, u32[]{:S(2)}, u32[]{:S(2)}) collective-permute-start(f32[2,64,128]{2,1,0:T(8,128)S(1)} %get-tuple-element.51), channel_id=1, source_target_pairs={{0,1},{1,0},{2,3},{3,2},{4,5},{5,4},{6,7},{7,6},{8,9},{9,8},{10,11... | collective-permute-start | bytes 196616 | tf_op jit(solution)/shard_map/ppermute | solution.py:254
  53.5 3.9 %collective-permute-start.9 = (f32[1,64,128]{2,1,0:T(8,128)S(1)}, f32[1,64,128]{2,1,0:T(8,128)S(1)}, u32[]{:S(2)}, u32[]{:S(2)}) collective-permute-start(f32[1,64,128]{2,1,0:T(8,128)S(1)} %slice_add_fusion), channel_id=1, source_target_pairs={{0,2},{1,3},{2,0},{3,1},{4,6},{5,7},{6,4},{7,5},{8,10},{9,11},{10,... | collective-permute-start | bytes 98312 | tf_op jit(solution)/shard_map/ppermute | solution.py:254
  57.4 1.3 %collective-permute-start.10 = (f32[64,128]{1,0:T(8,128)S(1)}, f32[64,128]{1,0:T(8,128)S(1)}, u32[]{:S(2)}, u32[]{:S(2)}) collective-permute-start(f32[64,128]{1,0:T(8,128)S(1)} %fusion.1), channel_id=1, source_target_pairs={{0,8},{8,0},{16,24},{24,16},{1,9},{9,1},{17,25},{25,17},{2,10},{10... | collective-permute-start | bytes 98312 | tf_op jit(solution)/shard_map/ppermute | solution.py:254
  58.7 3.9 %collective-permute-start.11 = (f32[64,128]{1,0:T(8,128)S(1)}, f32[64,128]{1,0:T(8,128)S(1)}, u32[]{:S(2)}, u32[]{:S(2)}) collective-permute-start(f32[64,128]{1,0:T(8,128)S(1)} %add.57.own), channel_id=1, source_target_pairs={{0,16},{8,24},{16,0},{24,8},{1,17},{9,25},{17,1},{25,9},{2,18},{10... | collective-permute-start | bytes 98312 | tf_op jit(solution)/shard_map/ppermute | solution.py:254
  63.7 3.9 %collective-permute-start.12 = (f32[4,16,128]{2,1,0:T(8,128)S(1)}, f32[4,16,128]{2,1,0:T(8,128)S(1)}, u32[]{:S(2)}, u32[]{:S(2)}) collective-permute-start(f32[4,16,128]{2,1,0:T(8,128)S(1)} %get-tuple-element.54), channel_id=1, source_target_pairs={{0,1},{1,0},{2,3},{3,2},{4,5},{5,4},{6,7},{7,6},{8,9},{9,8},{10,11... | collective-permute-start | bytes 98312 | tf_op jit(solution)/shard_map/ppermute | solution.py:254
  67.6 3.7 %collective-permute-start.13 = (f32[2,16,128]{2,1,0:T(8,128)S(1)}, f32[2,16,128]{2,1,0:T(8,128)S(1)}, u32[]{:S(2)}, u32[]{:S(2)}) collective-permute-start(f32[2,16,128]{2,1,0:T(8,128)S(1)} %slice_add_fusion.2), channel_id=1, source_target_pairs={{0,2},{1,3},{2,0},{3,1},{4,6},{5,7},{6,4},{7,5},{8,10},{9,11},{10,... | collective-permute-start | bytes 49160 | tf_op jit(solution)/shard_map/ppermute | solution.py:254
  71.3 4.5 %collective-permute-start.14 = (f32[1,16,128]{2,1,0:T(8,128)S(1)}, f32[1,16,128]{2,1,0:T(8,128)S(1)}, u32[]{:S(2)}, u32[]{:S(2)}) collective-permute-start(f32[1,16,128]{2,1,0:T(8,128)S(1)} %slice_add_fusion.3), channel_id=1, source_target_pairs={{0,4},{1,5},{2,6},{3,7},{4,0},{5,1},{6,2},{7,3},{8,12},{9,13},{10,... | collective-permute-start | bytes 24584 | tf_op jit(solution)/shard_map/ppermute | solution.py:254

commit v3 on v2

--- a/solution.py
+++ b/solution.py
@@ -1,4 +1,5 @@
 import functools
+import math
 
 import jax
 import jax.numpy as jnp
@@ -10,11 +11,19 @@
 
 NT = (((1,), (1,)), ((), ()))
 VMEM_LIMIT = 24 << 20
-AHEAD = 2
+AHEAD = 1
+CUT = (1, 2)
+GRAM_LAST = 1
+SCORE_LAST = 0
 
 
 def dot_nt(a, b):
     return lax.dot_general(a, b, NT, preferred_element_type=jnp.float32)
+
+
+def place(j, last):
+    level = min(lowest(j) if j else last, last)
+    return level, j >> (level + 1) if level < last else j >> last
 
 
 def lowest(j):
@@ -144,7 +153,7 @@
 
 
 def gram_kernel(n_blocks, here, tok_rows, has_prev, me, lengths, own, recv, *refs):
-    levels = n_blocks.bit_length()
+    levels = n_blocks.bit_length() - GRAM_LAST
     prevs = refs[:levels] if has_prev else ()
     outs, hi_rows, lo_rows = refs[-levels - 2 : -2], refs[-2], refs[-1]
     half = own.shape[0] // 4
@@ -178,20 +187,19 @@
         hi = hi_rows[pl.ds(start, width), :]
         lo = lo_rows[pl.ds(start, width), :]
         total = dot_nt(act_hi, hi) + (dot_nt(act_lo, hi) + dot_nt(act_hi, lo))
-        level = lowest(j) if j else levels - 1
-        at = j >> (level + 1) if j else 0
+        level, at = place(j, levels - 1)
         if has_prev:
             total = total + prevs[level][at]
         outs[level][at] = total
 
 
 def gram(me, lengths, own, recv, prevs, here, n_blocks, tok_rows):
-    levels = n_blocks.bit_length()
+    levels = n_blocks.bit_length() - GRAM_LAST
     half = own.shape[0] // 4
     piece = own.shape[1]
     prompts = lengths.shape[0]
     width = half * prompts // n_blocks
-    counts = [n_blocks >> (b + 1) for b in range(levels - 1)] + [1]
+    counts = [n_blocks >> (b + 1) for b in range(levels - 1)] + [1 << GRAM_LAST]
     vmem = pl.BlockSpec(memory_space=pltpu.VMEM)
     smem = pl.BlockSpec(memory_space=pltpu.SMEM)
     return pl.pallas_call(
@@ -207,10 +215,10 @@
     )(me, lengths, own, recv, *prevs)
 
 
-def score_kernel(n_ranks, me, lengths, own, recv, valid, *outs):
-    levels = n_ranks.bit_length()
+def score_kernel(n_ranks, me, lengths, own, valid, *outs):
+    levels = n_ranks.bit_length() - SCORE_LAST
     prompts = lengths.shape[0]
-    turned = (own[...] + recv[...]).T
+    turned = own[...].T
     rank = turned.shape[1]
     row = lax.broadcasted_iota(jnp.int32, (prompts, rank), 0)
     count = jnp.ones((prompts, rank), jnp.int32)
@@ -224,21 +232,20 @@
     width = valid.shape[0] // n_ranks
     for j in range(n_ranks):
         start = pl.multiple_of((j ^ me[0]) * width, width)
-        level = lowest(j) if j else levels - 1
-        at = j >> (level + 1) if j else 0
+        level, at = place(j, levels - 1)
         outs[level][at] = dot_nt(features, valid[pl.ds(start, width), :])
 
 
-def score(me, lengths, own, recv, valid, n_ranks):
-    levels = n_ranks.bit_length()
+def score(me, lengths, own, valid, n_ranks):
+    levels = n_ranks.bit_length() - SCORE_LAST
     prompts = lengths.shape[0]
     width = valid.shape[0] // n_ranks
-    counts = [n_ranks >> (b + 1) for b in range(levels - 1)] + [1]
+    counts = [n_ranks >> (b + 1) for b in range(levels - 1)] + [1 << SCORE_LAST]
     vmem = pl.BlockSpec(memory_space=pltpu.VMEM)
     smem = pl.BlockSpec(memory_space=pltpu.SMEM)
     return pl.pallas_call(
         functools.partial(score_kernel, n_ranks),
-        in_specs=[smem, smem, vmem, vmem, vmem],
+        in_specs=[smem, smem, vmem, vmem],
         out_specs=[vmem] * levels,
         out_shape=[jax.ShapeDtypeStruct((c, prompts, width), jnp.float32) for c in counts],
         name="score",
@@ -246,7 +253,7 @@
             flops=2 * prompts * valid.size, bytes_accessed=2 * valid.size, transcendentals=0
         ),
         compiler_params=pltpu.CompilerParams(vmem_limit_bytes=VMEM_LIMIT),
-    )(me, lengths, own, recv, valid)
+    )(me, lengths, own, valid)
 
 
 def swap(value, axis, bit):
@@ -255,15 +262,23 @@
 
 
 def halving(groups, axis):
-    for b in range(len(groups) - 1):
+    groups, last = list(groups), len(groups) - 1
+    for b in range(last):
         got = swap(groups[b], axis, b)
-        groups = list(groups)
-        for c in range(b + 1, len(groups) - 1):
-            step = 1 << (c - b)
-            first = 1 << (c - b - 1)
-            groups[c] = groups[c] + got[first::step]
-        groups[-1] = groups[-1] + got[:1]
-    return groups[-1]
+        for c in range(b + 1, last):
+            groups[c] = groups[c] + got[1 << (c - b - 1) :: 1 << (c - b)]
+        groups[last] = groups[last] + got[:: 1 << (last - b - 1)]
+    return groups[last]
+
+
+def direct(pieces):
+    dp, tensor = lax.axis_size("dp"), lax.axis_size("tensor")
+    total = pieces[0][0]
+    for value, dp_mask, mask in pieces[1:]:
+        move = dp_mask * tensor + mask
+        pairs = [(i, i ^ move) for i in range(dp * tensor)]
+        total = total + lax.ppermute(value, ("dp", "tensor"), pairs)
+    return total
 
 
 def plan(n_blocks):
@@ -281,8 +296,9 @@
     me = jnp.stack([lax.axis_index("tensor"), lax.axis_index("dp")]).astype(jnp.int32)
     rank = proj_in.shape[1]
     size = tok_rows // n_blocks
-    parts = [(0, size // 2), (size // 2, size // 2)]
-    strip = min(256, size // 2)
+    cut = size * CUT[0] // CUT[1]
+    parts = [(0, cut), (cut, size - cut)]
+    strip = min(256, math.gcd(cut, size))
     x, g, w_in, w_out = (
         pltpu.with_memory_space_constraint(v, pltpu.HBM)
         for v in (inputs, out_grads, proj_in.T, proj_out.T)
@@ -303,12 +319,18 @@
             else:
                 other = swap(own[: rank + rank // 2], "tensor", top)
                 grams = gram(me, lengths, own, other, grams, spot, n_blocks, tok_rows)
-    mine = halving(grams, "tensor")[0]
-    dp_bits = lax.axis_size("dp").bit_length() - 1
-    for b in range(dp_bits - 1):
-        mine = mine + swap(mine, "dp", b)
-    groups = score(me, lengths, mine, swap(mine, "dp", dp_bits - 1), valid_feats, n_ranks)
-    return halving(groups, "tensor")[0]
+    kept = halving(grams, "tensor")
+    dp_top = lax.axis_size("dp") // 2
+    for b in range(dp_top.bit_length() - 1):
+        kept = kept + swap(kept, "dp", b)
+    if GRAM_LAST:
+        z = n_blocks // 2
+        mine = direct([(kept[0], 0, 0), (kept[1], 0, z), (kept[0], dp_top, 0), (kept[1], dp_top, z)])
+    else:
+        mine = direct([(kept[0], 0, 0), (kept[0], dp_top, 0)])
+    kept = halving(score(me, lengths, mine, valid_feats, n_ranks), "tensor")
+    count = 1 << SCORE_LAST
+    return direct([(kept[i], 0, i * (n_ranks // count)) for i in range(count)])
 
 
 def solution(mesh):

time: 76.6 us -> 75 us (0.979)
  waiting for transfers between devices: 32.2 us -> 26.1 us
  starting transfers between devices: 19.2 us -> 23.3 us
    ppermute x15 -> x13, waiting for transfers between devices: 32.2 us -> 23.3 us  [swap(): return lax.ppermute(value, axis, [(i, i ^ 1 << bit) for i in range(count)])]
    ppermute x0 -> x3, starting transfers between devices: none -> 3.55 us  [direct(): total = total + lax.ppermute(value, ('dp', 'tensor'), pairs)]
    ppermute x0 -> x3, waiting for transfers between devices: none -> 2.89 us  [direct(): total = total + lax.ppermute(value, ('dp', 'tensor'), pairs)]
    ppermute x15 -> x13, starting transfers between devices: 19.2 us -> 19.8 us  [swap(): return lax.ppermute(value, axis, [(i, i ^ 1 << bit) for i in range(count)])]
  transfers between devices with their start and end apart: 15 -> 16, of which waited for: 12 -> 12; matrix products, arithmetic and copies ran while one was open for 0% -> 0% of each run, Pallas kernels for 22% -> 23%
where the time goes in v3:
time: 75 us; the launch traced here: 74.9 us
  waiting for transfers between devices  26.1 us (35%)
  Pallas kernels  24.3 us (32%)
  starting transfers between devices  23.3 us (31%)
  other arithmetic  0.9 us (1%)
    ppermute x13, waiting for transfers between devices, swap(): return lax.ppermute(value, axis, [(i, i ^ 1 << bit) for i in range(count)])  23.3 us
    pallas_call x4, Pallas kernels, project(): pl.pallas_call(functools.partial(project_kernel, first, n_blocks, here, a...  20.6 us
    ppermute x13, starting transfers between devices, swap(): return lax.ppermute(value, axis, [(i, i ^ 1 << bit) for i in range(count)])  19.8 us
    ppermute x3, starting transfers between devices, direct(): total = total + lax.ppermute(value, ('dp', 'tensor'), pairs)  3.55 us
    ppermute x3, waiting for transfers between devices, direct(): total = total + lax.ppermute(value, ('dp', 'tensor'), pairs)  2.89 us
    pallas_call x2, Pallas kernels, gram(): pl.pallas_call(functools.partial(gram_kernel, n_blocks, here, tok_rows, b...  2.7 us
  transfers between devices with their start and end apart: 16, of which 12 were waited for; matrix products, arithmetic and copies ran while one was open for 0% of the time, Pallas kernels for 23%

profile of v3, /device:TPU:0, one launch (start us, length us, event | category | flops | bytes accessed | tf_op | source)
XLA Modules:
  0.0 74.9 jit_solution(17030839835229795061)
XLA Ops:
  0.0 0.1 pad_add_fusion.me
  0.1 4.5 %shard_map.64 = (f32[128,512]{1,0:T(8,128)S(1)}, bf16[6,256,3584]{2,1,0:T(8,128)(2,1)S(1)}, bf16[6,256,1024]{2,1,0:T(8,128)(2,1)S(1)}, bf16[64,3584]{1,0:T(8,128)(2,1)S(1)}, bf16[64,1024]{1,0:T(8,128)(2,1)S(1)}) custom-call(s32[2]{0:T(128)S(1)} %pad_add_fusion.me, bf16[4096,3584]{1,0:T(8,128)(2,1)} %x.7, bf16[4096,1024]{1,0:T(8,128)(2,1)} %g.7, ...), custom_call_target="tpu_custom_call" | custom-call | flops 603979776 | bytes 4718592 | tf_op jit(solution)/shard_map/pallas_call | solution.py:140
  4.6 3.0 %collective-permute-start.5 = (f32[128,512]{1,0:T(8,128)S(1)}, f32[128,512]{1,0:T(8,128)S(1)}, u32[]{:S(2)}, u32[]{:S(2)}) collective-permute-start(f32[128,512]{1,0:T(8,128)S(1)} %get-tuple-element.44), channel_id=1, source_target_pairs={{0,1},{1,0},{2,3},{3,2},{4,5},{5,4},{6,7},{7,6},{8,9},{9,8},{10,11... | collective-permute-start | bytes 786440 | tf_op jit(solution)/shard_map/ppermute | solution.py:261
  7.6 6.5 %shard_map.65 = (f32[128,512]{1,0:T(8,128)S(1)}, f32[128,512]{1,0:T(8,128)S(1)}, f32[128,512]{1,0:T(8,128)S(1)}, bf16[6,256,3584]{2,1,0:T(8,128)(2,1)S(1)}, bf16...) custom-call(s32[2]{0:T(128)S(1)} %pad_add_fusion.me, ...), custom_call_target="tpu_custom_call", output_to_operand_aliasing={{5}: (5, {}), {6}: (6, {})} | custom-call | flops 1811939328 | bytes 14155776 | tf_op jit(solution)/shard_map/pallas_call | solution.py:140
  14.1 0.1 collective-permute-start.1
  14.2 2.0 %collective-permute-start.4 = (f32[128,512]{1,0:T(8,128)S(1)}, f32[128,512]{1,0:T(8,128)S(1)}, u32[]{:S(2)}, u32[]{:S(2)}) collective-permute-start(f32[128,512]{1,0:T(8,128)S(1)} %get-tuple-element.42), channel_id=1, source_target_pairs={{0,1},{1,0},{2,3},{3,2},{4,5},{5,4},{6,7},{7,6},{8,9},{9,8},{10,11... | collective-permute-start | bytes 786440 | tf_op jit(solution)/shard_map/ppermute | solution.py:261
  16.2 0.0 collective-permute-done.5
  16.3 1.6 %collective-permute-start.6 = (f32[128,512]{1,0:T(8,128)S(1)}, f32[128,512]{1,0:T(8,128)S(1)}, u32[]{:S(2)}, u32[]{:S(2)}) collective-permute-start(f32[128,512]{1,0:T(8,128)S(1)} %add.55), channel_id=1, source_target_pairs={{0,2},{1,3},{2,0},{3,1},{4,6},{5,7},{6,4},{7,5},{8,10},{9,11},{10,... | collective-permute-start | bytes 786440 | tf_op jit(solution)/shard_map/ppermute | solution.py:261
  17.9 6.5 %shard_map.66 = (f32[128,512]{1,0:T(8,128)S(1)}, f32[128,512]{1,0:T(8,128)S(1)}, f32[128,512]{1,0:T(8,128)S(1)}, bf16[2,256,3584]{2,1,0:T(8,128)(2,1)S(1)}, bf16...) custom-call(s32[2]{0:T(128)S(1)} %pad_add_fusion.me, ...), custom_call_target="tpu_custom_call", output_to_operand_aliasing={{5}: (5, {}), {6}: (6, {})} | custom-call | flops 1811939328 | bytes 14155776 | tf_op jit(solution)/shard_map/pallas_call | solution.py:140
  24.4 0.6 collective-permute-start
  25.0 0.0 collective-permute-done.1
  25.0 0.1 collective-permute-start.2
  25.1 0.0 copy-start.1
  25.1 0.0 copy-start
  25.2 3.0 %shard_map.67 = (f32[128,512]{1,0:T(8,128)S(1)}, bf16[2,256,3584]{2,1,0:T(8,128)(2,1)S(1)}, bf16[2,256,1024]{2,1,0:T(8,128)(2,1)S(1)}) custom-call(s32[2]{0:T(128)S(1)} %pad_add_fusion.me, bf16[4096,3584]{1,0:T(8,128)(2,1)} %x.7, bf16[4096,1024]{1,0:T(8,128)(2,1)} %g.7, ...), custom_call_target="tpu_custom_call", output_to_operand_aliasing={{1}: (5, {}), {2}: (6, {})} | custom-call | flops 603979776 | bytes 4718592 | tf_op jit(solution)/shard_map/pallas_call | solution.py:140
  28.2 0.8 %collective-permute-done.4 = f32[128,512]{1,0:T(8,128)S(1)} collective-permute-done((f32[128,512]{1,0:T(8,128)S(1)}, f32[128,512]{1,0:T(8,128)S(1)}, u32[]{:S(2)}, u32[]{:S(2)}) %collective-permute-start.4) | collective-permute-done | bytes 262176 | tf_op jit(solution)/shard_map/ppermute | solution.py:261
  29.0 0.0 collective-permute-done.6
  29.0 0.1 add_add_fusion.own
  29.1 2.7 %collective-permute-start.7 = (f32[96,512]{1,0:T(8,128)S(1)}, f32[96,512]{1,0:T(8,128)S(1)}, u32[]{:S(2)}, u32[]{:S(2)}) collective-permute-start(f32[96,512]{1,0:T(8,128)S(1)} %slice.43), channel_id=1, source_target_pairs={{0,4},{1,5},{2,6},{3,7},{4,0},{5,1},{6,2},{7,3},{8,12},{9,13},{10,... | collective-permute-start | bytes 589832 | tf_op jit(solution)/shard_map/ppermute | solution.py:261
  31.7 1.5 %collective-permute-done = f32[128,512]{1,0:T(8,128)S(1)} collective-permute-done((f32[128,512]{1,0:T(8,128)S(1)}, f32[128,512]{1,0:T(8,128)S(1)}, u32[]{:S(2)}, u32[]{:S(2)}) %collective-permute-start) | collective-permute-done | bytes 262176 | tf_op jit(solution)/shard_map/ppermute | solution.py:261
  33.2 0.9 %collective-permute-done.2 = f32[128,512]{1,0:T(8,128)S(1)} collective-permute-done((f32[128,512]{1,0:T(8,128)S(1)}, f32[128,512]{1,0:T(8,128)S(1)}, u32[]{:S(2)}, u32[]{:S(2)}) %collective-permute-start.2) | collective-permute-done | bytes 262176 | tf_op jit(solution)/shard_map/ppermute | solution.py:261
  34.1 0.1 add_add_fusion.1.own
  34.2 2.4 %collective-permute-start.3 = (f32[96,512]{1,0:T(8,128)S(1)}, f32[96,512]{1,0:T(8,128)S(1)}, u32[]{:S(2)}, u32[]{:S(2)}) collective-permute-start(f32[96,512]{1,0:T(8,128)S(1)} %slice.42), channel_id=1, source_target_pairs={{0,4},{1,5},{2,6},{3,7},{4,0},{5,1},{6,2},{7,3},{8,12},{9,13},{10,... | collective-permute-start | bytes 589832 | tf_op jit(solution)/shard_map/ppermute | solution.py:261
  36.6 7.6 %collective-permute-done.7.recv = f32[96,512]{1,0:T(8,128)S(1)} collective-permute-done((f32[96,512]{1,0:T(8,128)S(1)}, f32[96,512]{1,0:T(8,128)S(1)}, u32[]{:S(2)}, u32[]{:S(2)}) %collective-permute-start.7) | collective-permute-done | bytes 196640 | tf_op jit(solution)/shard_map/ppermute | solution.py:261
  44.2 0.0 copy-done.1
  44.2 1.3 %shard_map.68 = (f32[2,64,128]{2,1,0:T(8,128)S(1)}, f32[2,64,128]{2,1,0:T(8,128)S(1)}) custom-call(s32[2]{0:T(128)S(1)} %pad_add_fusion.me, s32[16]{0:T(128)S(1)} %copy-done.1, f32[128,512]{1,0:T(8,128)S(1)} %add_add_fusion.own, f32[96,512]{1,0:T(8,128)S(1)} %collective-permute-done.7.recv), custom_call_target="tpu_custom_call" | custom-call | flops 100663296 | bytes 524288 | tf_op jit(solution)/shard_map/pallas_call | solution.py:205
  45.5 1.8 %collective-permute-done.3.recv = f32[96,512]{1,0:T(8,128)S(1)} collective-permute-done((f32[96,512]{1,0:T(8,128)S(1)}, f32[96,512]{1,0:T(8,128)S(1)}, u32[]{:S(2)}, u32[]{:S(2)}) %collective-permute-start.3) | collective-permute-done | bytes 196640 | tf_op jit(solution)/shard_map/ppermute | solution.py:261
  47.3 1.4 %shard_map.69 = (f32[2,64,128]{2,1,0:T(8,128)S(1)}, f32[2,64,128]{2,1,0:T(8,128)S(1)}) custom-call(s32[2]{0:T(128)S(1)} %pad_add_fusion.me, s32[16]{0:T(128)S(1)} %copy-done.1, f32[128,512]{1,0:T(8,128)S(1)} %add_add_fusion.1.own, f32[96,512]{1,0:T(8,128)S(1)} %collective-permute-done.3.recv, f32[2,64,128]{2,1,0:T(8,128)S(1)} %get-tuple-element.45.refs_0_, ...), custom_call_target="tpu_custom_call" | custom-call | flops 100663296 | bytes 524288 | tf_op jit(solution)/shard_map/pallas_call | solution.py:205
  48.7 1.6 %collective-permute-start.8 = (f32[2,64,128]{2,1,0:T(8,128)S(1)}, f32[2,64,128]{2,1,0:T(8,128)S(1)}, u32[]{:S(2)}, u32[]{:S(2)}) collective-permute-start(f32[2,64,128]{2,1,0:T(8,128)S(1)} %get-tuple-element.48), channel_id=1, source_target_pairs={{0,1},{1,0},{2,3},{3,2},{4,5},{5,4},{6,7},{7,6},{8,9},{9,8},{10,11... | collective-permute-start | bytes 196616 | tf_op jit(solution)/shard_map/ppermute | solution.py:261
  50.3 2.7 %collective-permute-done.8 = f32[2,64,128]{2,1,0:T(8,128)S(1)} collective-permute-done((f32[2,64,128]{2,1,0:T(8,128)S(1)}, f32[2,64,128]{2,1,0:T(8,128)S(1)}, u32[]{:S(2)}, u32[]{:S(2)}) %collective-permute-start.8) | collective-permute-done | bytes 65568 | tf_op jit(solution)/shard_map/ppermute | solution.py:261
  53.0 0.1 collective-permute-start.9
  53.1 1.2 %collective-permute-done.9 = f32[2,64,128]{2,1,0:T(8,128)S(1)} collective-permute-done((f32[2,64,128]{2,1,0:T(8,128)S(1)}, f32[2,64,128]{2,1,0:T(8,128)S(1)}, u32[]{:S(2)}, u32[]{:S(2)}) %collective-permute-start.9) | collective-permute-done | bytes 65568 | tf_op jit(solution)/shard_map/ppermute | solution.py:261
  54.4 1.6 %collective-permute-start.11 = (f32[64,128]{1,0:T(8,128)S(1)}, f32[64,128]{1,0:T(8,128)S(1)}, u32[]{:S(2)}, u32[]{:S(2)}) collective-permute-start(f32[64,128]{1,0:T(8,128)S(1)} %get-tuple-element.53), channel_id=1, source_target_pairs={{0,16},{1,17},{2,18},{3,19},{4,20},{5,21},{6,22},{7,23},{8,24},{9,... | collective-permute-start | bytes 98312 | tf_op jit(solution)/shard_map/ppermute | solution.py:280
  56.0 0.6 collective-permute-start.12
  56.6 1.3 %collective-permute-start.10 = (f32[64,128]{1,0:T(8,128)S(1)}, f32[64,128]{1,0:T(8,128)S(1)}, u32[]{:S(2)}, u32[]{:S(2)}) collective-permute-start(f32[64,128]{1,0:T(8,128)S(1)} %get-tuple-element.54), channel_id=1, source_target_pairs={{0,2},{1,3},{2,0},{3,1},{4,6},{5,7},{6,4},{7,5},{8,10},{9,11},{10,... | collective-permute-start | bytes 98312 | tf_op jit(solution)/shard_map/ppermute | solution.py:280
  57.9 0.4 collective-permute-done.11
  58.4 2.5 %collective-permute-done.12 = f32[64,128]{1,0:T(8,128)S(1)} collective-permute-done((f32[64,128]{1,0:T(8,128)S(1)}, f32[64,128]{1,0:T(8,128)S(1)}, u32[]{:S(2)}, u32[]{:S(2)}) %collective-permute-start.12) | collective-permute-done | bytes 32800 | tf_op jit(solution)/shard_map/ppermute | solution.py:280
  60.8 0.0 collective-permute-done.10
  60.9 0.0 copy-done
  60.9 1.0 %score.1 = (f32[4,16,128]{2,1,0:T(8,128)S(1)}, f32[2,16,128]{2,1,0:T(8,128)S(1)}, f32[1,16,128]{2,1,0:T(8,128)S(1)}, f32[1,16,128]{2,1,0:T(8,128)S(1)}) custom-call(s32[2]{0:T(128)S(1)} %pad_add_fusion.me, s32[16]{0:T(128)S(1)} %copy-done.1, f32[64,128]{1,0:T(8,128)S(1)} %add_add_fusion.2.own, bf16[1024,512]{1,0:T(8,128)(2,1)S(1)} %copy-done), custom_call_target="tpu_custom_call" | custom-call | flops 16777216 | bytes 1048576 | tf_op jit(solution)/shard_map/score/pallas_call | solution.py:246
  61.9 1.5 %collective-permute-start.13 = (f32[4,16,128]{2,1,0:T(8,128)S(1)}, f32[4,16,128]{2,1,0:T(8,128)S(1)}, u32[]{:S(2)}, u32[]{:S(2)}) collective-permute-start(f32[4,16,128]{2,1,0:T(8,128)S(1)} %get-tuple-element.50), channel_id=1, source_target_pairs={{0,1},{1,0},{2,3},{3,2},{4,5},{5,4},{6,7},{7,6},{8,9},{9,8},{10,11... | collective-permute-start | bytes 98312 | tf_op jit(solution)/shard_map/ppermute | solution.py:261
  63.4 2.4 %collective-permute-done.13 = f32[4,16,128]{2,1,0:T(8,128)S(1)} collective-permute-done((f32[4,16,128]{2,1,0:T(8,128)S(1)}, f32[4,16,128]{2,1,0:T(8,128)S(1)}, u32[]{:S(2)}, u32[]{:S(2)}) %collective-permute-start.13) | collective-permute-done | bytes 32800 | tf_op jit(solution)/shard_map/ppermute | solution.py:261
  65.8 1.0 %collective-permute-start.14 = (f32[2,16,128]{2,1,0:T(8,128)S(1)}, f32[2,16,128]{2,1,0:T(8,128)S(1)}, u32[]{:S(2)}, u32[]{:S(2)}) collective-permute-start(f32[2,16,128]{2,1,0:T(8,128)S(1)} %slice_add_fusion), channel_id=1, source_target_pairs={{0,2},{1,3},{2,0},{3,1},{4,6},{5,7},{6,4},{7,5},{8,10},{9,11},{10,... | collective-permute-start | bytes 49160 | tf_op jit(solution)/shard_map/ppermute | solution.py:261
  66.9 2.7 %collective-permute-done.14 = f32[2,16,128]{2,1,0:T(8,128)S(1)} collective-permute-done((f32[2,16,128]{2,1,0:T(8,128)S(1)}, f32[2,16,128]{2,1,0:T(8,128)S(1)}, u32[]{:S(2)}, u32[]{:S(2)}) %collective-permute-start.14) | collective-permute-done | bytes 16416 | tf_op jit(solution)/shard_map/ppermute | solution.py:261
  69.6 3.0 %collective-permute-start.15 = (f32[1,16,128]{2,1,0:T(8,128)S(1)}, f32[1,16,128]{2,1,0:T(8,128)S(1)}, u32[]{:S(2)}, u32[]{:S(2)}) collective-permute-start(f32[1,16,128]{2,1,0:T(8,128)S(1)} %slice_add_fusion.1), channel_id=1, source_target_pairs={{0,4},{1,5},{2,6},{3,7},{4,0},{5,1},{6,2},{7,3},{8,12},{9,13},{10,... | collective-permute-start | bytes 24584 | tf_op jit(solution)/shard_map/ppermute | solution.py:261
  72.6 1.6 %collective-permute-done.15 = f32[1,16,128]{2,1,0:T(8,128)S(1)} collective-permute-done((f32[1,16,128]{2,1,0:T(8,128)S(1)}, f32[1,16,128]{2,1,0:T(8,128)S(1)}, u32[]{:S(2)}, u32[]{:S(2)}) %collective-permute-start.15) | collective-permute-done | bytes 8224 | tf_op jit(solution)/shard_map/ppermute | solution.py:261
  74.3 0.6 fusion.1
  (10 shorter events, 0.1 us)
Async XLA Ops:
  4.6 11.7 %collective-permute-start.5 = (f32[128,512]{1,0:T(8,128)S(1)}, f32[128,512]{1,0:T(8,128)S(1)}, u32[]{:S(2)}, u32[]{:S(2)}) collective-permute-start(f32[128,512]{1,0:T(8,128)S(1)} %get-tuple-element.44), channel_id=1, source_target_pairs={{0,1},{1,0},{2,3},{3,2},{4,5},{5,4},{6,7},{7,6},{8,9},{9,8},{10,11... | collective-permute-start | bytes 786440 | tf_op jit(solution)/shard_map/ppermute | solution.py:261
  14.1 10.9 %collective-permute-start.1 = (f32[128,512]{1,0:T(8,128)S(1)}, f32[128,512]{1,0:T(8,128)S(1)}, u32[]{:S(2)}, u32[]{:S(2)}) collective-permute-start(f32[128,512]{1,0:T(8,128)S(1)} %get-tuple-element.40), channel_id=1, source_target_pairs={{0,1},{1,0},{2,3},{3,2},{4,5},{5,4},{6,7},{7,6},{8,9},{9,8},{10,11... | collective-permute-start | bytes 786440 | tf_op jit(solution)/shard_map/ppermute | solution.py:261
  14.2 14.8 %collective-permute-start.4 = (f32[128,512]{1,0:T(8,128)S(1)}, f32[128,512]{1,0:T(8,128)S(1)}, u32[]{:S(2)}, u32[]{:S(2)}) collective-permute-start(f32[128,512]{1,0:T(8,128)S(1)} %get-tuple-element.42), channel_id=1, source_target_pairs={{0,1},{1,0},{2,3},{3,2},{4,5},{5,4},{6,7},{7,6},{8,9},{9,8},{10,11... | collective-permute-start | bytes 786440 | tf_op jit(solution)/shard_map/ppermute | solution.py:261
  16.3 12.7 %collective-permute-start.6 = (f32[128,512]{1,0:T(8,128)S(1)}, f32[128,512]{1,0:T(8,128)S(1)}, u32[]{:S(2)}, u32[]{:S(2)}) collective-permute-start(f32[128,512]{1,0:T(8,128)S(1)} %add.55), channel_id=1, source_target_pairs={{0,2},{1,3},{2,0},{3,1},{4,6},{5,7},{6,4},{7,5},{8,10},{9,11},{10,... | collective-permute-start | bytes 786440 | tf_op jit(solution)/shard_map/ppermute | solution.py:261
  24.4 8.8 %collective-permute-start = (f32[128,512]{1,0:T(8,128)S(1)}, f32[128,512]{1,0:T(8,128)S(1)}, u32[]{:S(2)}, u32[]{:S(2)}) collective-permute-start(f32[128,512]{1,0:T(8,128)S(1)} %get-tuple-element.38), channel_id=1, source_target_pairs={{0,1},{1,0},{2,3},{3,2},{4,5},{5,4},{6,7},{7,6},{8,9},{9,8},{10,11... | collective-permute-start | bytes 786440 | tf_op jit(solution)/shard_map/ppermute | solution.py:261
  25.0 9.1 %collective-permute-start.2 = (f32[128,512]{1,0:T(8,128)S(1)}, f32[128,512]{1,0:T(8,128)S(1)}, u32[]{:S(2)}, u32[]{:S(2)}) collective-permute-start(f32[128,512]{1,0:T(8,128)S(1)} %add.52), channel_id=1, source_target_pairs={{0,2},{1,3},{2,0},{3,1},{4,6},{5,7},{6,4},{7,5},{8,10},{9,11},{10,... | collective-permute-start | bytes 786440 | tf_op jit(solution)/shard_map/ppermute | solution.py:261
  25.1 19.1 %copy-start.1 = (s32[16]{0:T(128)S(1)}, s32[16]{0:T(128)}, u32[]{:S(2)}) copy-start(s32[16]{0:T(128)} %lengths.5) | copy-start | bytes 196
  25.1 35.7 %copy-start = (bf16[1024,512]{1,0:T(8,128)(2,1)S(1)}, bf16[1024,512]{1,0:T(8,128)(2,1)}, u32[]{:S(2)}) copy-start(bf16[1024,512]{1,0:T(8,128)(2,1)} %valid.1) | copy-start | bytes 3145732
  29.1 15.1 %collective-permute-start.7 = (f32[96,512]{1,0:T(8,128)S(1)}, f32[96,512]{1,0:T(8,128)S(1)}, u32[]{:S(2)}, u32[]{:S(2)}) collective-permute-start(f32[96,512]{1,0:T(8,128)S(1)} %slice.43), channel_id=1, source_target_pairs={{0,4},{1,5},{2,6},{3,7},{4,0},{5,1},{6,2},{7,3},{8,12},{9,13},{10,... | collective-permute-start | bytes 589832 | tf_op jit(solution)/shard_map/ppermute | solution.py:261
  34.2 13.1 %collective-permute-start.3 = (f32[96,512]{1,0:T(8,128)S(1)}, f32[96,512]{1,0:T(8,128)S(1)}, u32[]{:S(2)}, u32[]{:S(2)}) collective-permute-start(f32[96,512]{1,0:T(8,128)S(1)} %slice.42), channel_id=1, source_target_pairs={{0,4},{1,5},{2,6},{3,7},{4,0},{5,1},{6,2},{7,3},{8,12},{9,13},{10,... | collective-permute-start | bytes 589832 | tf_op jit(solution)/shard_map/ppermute | solution.py:261
  48.7 4.3 %collective-permute-start.8 = (f32[2,64,128]{2,1,0:T(8,128)S(1)}, f32[2,64,128]{2,1,0:T(8,128)S(1)}, u32[]{:S(2)}, u32[]{:S(2)}) collective-permute-start(f32[2,64,128]{2,1,0:T(8,128)S(1)} %get-tuple-element.48), channel_id=1, source_target_pairs={{0,1},{1,0},{2,3},{3,2},{4,5},{5,4},{6,7},{7,6},{8,9},{9,8},{10,11... | collective-permute-start | bytes 196616 | tf_op jit(solution)/shard_map/ppermute | solution.py:261
  53.0 1.3 %collective-permute-start.9 = (f32[2,64,128]{2,1,0:T(8,128)S(1)}, f32[2,64,128]{2,1,0:T(8,128)S(1)}, u32[]{:S(2)}, u32[]{:S(2)}) collective-permute-start(f32[2,64,128]{2,1,0:T(8,128)S(1)} %add.57), channel_id=1, source_target_pairs={{0,8},{8,0},{16,24},{24,16},{1,9},{9,1},{17,25},{25,17},{2,10},{10... | collective-permute-start | bytes 196616 | tf_op jit(solution)/shard_map/ppermute | solution.py:261
  54.4 4.0 %collective-permute-start.11 = (f32[64,128]{1,0:T(8,128)S(1)}, f32[64,128]{1,0:T(8,128)S(1)}, u32[]{:S(2)}, u32[]{:S(2)}) collective-permute-start(f32[64,128]{1,0:T(8,128)S(1)} %get-tuple-element.53), channel_id=1, source_target_pairs={{0,16},{1,17},{2,18},{3,19},{4,20},{5,21},{6,22},{7,23},{8,24},{9,... | collective-permute-start | bytes 98312 | tf_op jit(solution)/shard_map/ppermute | solution.py:280
  56.0 4.8 %collective-permute-start.12 = (f32[64,128]{1,0:T(8,128)S(1)}, f32[64,128]{1,0:T(8,128)S(1)}, u32[]{:S(2)}, u32[]{:S(2)}) collective-permute-start(f32[64,128]{1,0:T(8,128)S(1)} %get-tuple-element.54), channel_id=1, source_target_pairs={{0,18},{1,19},{2,16},{3,17},{4,22},{5,23},{6,20},{7,21},{8,26},{9,... | collective-permute-start | bytes 98312 | tf_op jit(solution)/shard_map/ppermute | solution.py:280
  56.6 4.2 %collective-permute-start.10 = (f32[64,128]{1,0:T(8,128)S(1)}, f32[64,128]{1,0:T(8,128)S(1)}, u32[]{:S(2)}, u32[]{:S(2)}) collective-permute-start(f32[64,128]{1,0:T(8,128)S(1)} %get-tuple-element.54), channel_id=1, source_target_pairs={{0,2},{1,3},{2,0},{3,1},{4,6},{5,7},{6,4},{7,5},{8,10},{9,11},{10,... | collective-permute-start | bytes 98312 | tf_op jit(solution)/shard_map/ppermute | solution.py:280
  61.9 3.9 %collective-permute-start.13 = (f32[4,16,128]{2,1,0:T(8,128)S(1)}, f32[4,16,128]{2,1,0:T(8,128)S(1)}, u32[]{:S(2)}, u32[]{:S(2)}) collective-permute-start(f32[4,16,128]{2,1,0:T(8,128)S(1)} %get-tuple-element.50), channel_id=1, source_target_pairs={{0,1},{1,0},{2,3},{3,2},{4,5},{5,4},{6,7},{7,6},{8,9},{9,8},{10,11... | collective-permute-start | bytes 98312 | tf_op jit(solution)/shard_map/ppermute | solution.py:261
  65.8 3.7 %collective-permute-start.14 = (f32[2,16,128]{2,1,0:T(8,128)S(1)}, f32[2,16,128]{2,1,0:T(8,128)S(1)}, u32[]{:S(2)}, u32[]{:S(2)}) collective-permute-start(f32[2,16,128]{2,1,0:T(8,128)S(1)} %slice_add_fusion), channel_id=1, source_target_pairs={{0,2},{1,3},{2,0},{3,1},{4,6},{5,7},{6,4},{7,5},{8,10},{9,11},{10,... | collective-permute-start | bytes 49160 | tf_op jit(solution)/shard_map/ppermute | solution.py:261
  69.6 4.7 %collective-permute-start.15 = (f32[1,16,128]{2,1,0:T(8,128)S(1)}, f32[1,16,128]{2,1,0:T(8,128)S(1)}, u32[]{:S(2)}, u32[]{:S(2)}) collective-permute-start(f32[1,16,128]{2,1,0:T(8,128)S(1)} %slice_add_fusion.1), channel_id=1, source_target_pairs={{0,4},{1,5},{2,6},{3,7},{4,0},{5,1},{6,2},{7,3},{8,12},{9,13},{10,... | collective-permute-start | bytes 24584 | tf_op jit(solution)/shard_map/ppermute | solution.py:261

commit v4 on v3

--- a/solution.py
+++ b/solution.py
@@ -155,7 +155,8 @@
 def gram_kernel(n_blocks, here, tok_rows, has_prev, me, lengths, own, recv, *refs):
     levels = n_blocks.bit_length() - GRAM_LAST
     prevs = refs[:levels] if has_prev else ()
-    outs, hi_rows, lo_rows = refs[-levels - 2 : -2], refs[-2], refs[-1]
+    outs = refs[-levels - 3 : -3]
+    hi_rows, lo_rows, placed = refs[-3:]
     half = own.shape[0] // 4
     piece = own.shape[1]
     prompts = lengths.shape[0]
@@ -182,11 +183,12 @@
         hi_rows[i * prompts : (i + 1) * prompts] = line_hi
         lo_rows[i * prompts : (i + 1) * prompts] = (line - line_hi.astype(jnp.float32)).astype(jnp.bfloat16)
     width = half * prompts // n_blocks
+    both = dot_nt(jnp.concatenate([act_hi, act_lo], axis=0), hi_rows[...])
+    sums = both[: 2 * half] + (both[2 * half :] + dot_nt(act_hi, lo_rows[...]))
+    for s in range(n_blocks):
+        placed[s ^ which] = sums[:, s * width : (s + 1) * width]
     for j in range(n_blocks):
-        start = pl.multiple_of((j ^ which) * width, width)
-        hi = hi_rows[pl.ds(start, width), :]
-        lo = lo_rows[pl.ds(start, width), :]
-        total = dot_nt(act_hi, hi) + (dot_nt(act_lo, hi) + dot_nt(act_hi, lo))
+        total = placed[j]
         level, at = place(j, levels - 1)
         if has_prev:
             total = total + prevs[level][at]
@@ -207,7 +209,8 @@
         in_specs=[smem, smem] + [vmem] * (2 + len(prevs)),
         out_specs=[vmem] * levels,
         out_shape=[jax.ShapeDtypeStruct((c, 2 * half, width), jnp.float32) for c in counts],
-        scratch_shapes=[pltpu.VMEM((half * prompts, piece), jnp.bfloat16)] * 2,
+        scratch_shapes=[pltpu.VMEM((half * prompts, piece), jnp.bfloat16)] * 2
+        + [pltpu.VMEM((n_blocks, 2 * half, width), jnp.float32)],
         cost_estimate=pl.CostEstimate(
             flops=12 * half * half * prompts * piece, bytes_accessed=8 * own.size, transcendentals=0
         ),

time: 75 us -> 74.6 us (level)
  no operation moved by 1% of the time
where the time goes in v4:
time: 74.6 us; the launch traced here: 74.5 us
  waiting for transfers between devices  26.4 us (35%)
  Pallas kernels  23.6 us (32%)
  starting transfers between devices  23.3 us (31%)
  other arithmetic  0.9 us (1%)
    ppermute x13, waiting for transfers between devices, swap(): return lax.ppermute(value, axis, [(i, i ^ 1 << bit) for i in range(count)])  23.5 us
    pallas_call x4, Pallas kernels, project(): pl.pallas_call(functools.partial(project_kernel, first, n_blocks, here, a...  20.6 us
    ppermute x13, starting transfers between devices, swap(): return lax.ppermute(value, axis, [(i, i ^ 1 << bit) for i in range(count)])  19.8 us
    ppermute x3, starting transfers between devices, direct(): total = total + lax.ppermute(value, ('dp', 'tensor'), pairs)  3.55 us
    ppermute x3, waiting for transfers between devices, direct(): total = total + lax.ppermute(value, ('dp', 'tensor'), pairs)  2.9 us
    pallas_call x2, Pallas kernels, gram(): pl.pallas_call(functools.partial(gram_kernel, n_blocks, here, tok_rows, b...  2.05 us
  transfers between devices with their start and end apart: 16, of which 12 were waited for; matrix products, arithmetic and copies ran while one was open for 0% of the time, Pallas kernels for 23%

profile of v4, /device:TPU:0, one launch (start us, length us, event | category | flops | bytes accessed | tf_op | source)
XLA Modules:
  0.0 74.5 jit_solution(3369281644637846425)
XLA Ops:
  0.0 0.1 pad_add_fusion.me
  0.1 4.5 %shard_map.64 = (f32[128,512]{1,0:T(8,128)S(1)}, bf16[6,256,3584]{2,1,0:T(8,128)(2,1)S(1)}, bf16[6,256,1024]{2,1,0:T(8,128)(2,1)S(1)}, bf16[64,3584]{1,0:T(8,128)(2,1)S(1)}, bf16[64,1024]{1,0:T(8,128)(2,1)S(1)}) custom-call(s32[2]{0:T(128)S(1)} %pad_add_fusion.me, bf16[4096,3584]{1,0:T(8,128)(2,1)} %x.7, bf16[4096,1024]{1,0:T(8,128)(2,1)} %g.7, ...), custom_call_target="tpu_custom_call" | custom-call | flops 603979776 | bytes 4718592 | tf_op jit(solution)/shard_map/pallas_call | solution.py:140
  4.6 3.0 %collective-permute-start.5 = (f32[128,512]{1,0:T(8,128)S(1)}, f32[128,512]{1,0:T(8,128)S(1)}, u32[]{:S(2)}, u32[]{:S(2)}) collective-permute-start(f32[128,512]{1,0:T(8,128)S(1)} %get-tuple-element.44), channel_id=1, source_target_pairs={{0,1},{1,0},{2,3},{3,2},{4,5},{5,4},{6,7},{7,6},{8,9},{9,8},{10,11... | collective-permute-start | bytes 786440 | tf_op jit(solution)/shard_map/ppermute | solution.py:264
  7.6 6.5 %shard_map.65 = (f32[128,512]{1,0:T(8,128)S(1)}, f32[128,512]{1,0:T(8,128)S(1)}, f32[128,512]{1,0:T(8,128)S(1)}, bf16[6,256,3584]{2,1,0:T(8,128)(2,1)S(1)}, bf16...) custom-call(s32[2]{0:T(128)S(1)} %pad_add_fusion.me, ...), custom_call_target="tpu_custom_call", output_to_operand_aliasing={{5}: (5, {}), {6}: (6, {})} | custom-call | flops 1811939328 | bytes 14155776 | tf_op jit(solution)/shard_map/pallas_call | solution.py:140
  14.1 0.1 collective-permute-start.1
  14.2 2.0 %collective-permute-start.4 = (f32[128,512]{1,0:T(8,128)S(1)}, f32[128,512]{1,0:T(8,128)S(1)}, u32[]{:S(2)}, u32[]{:S(2)}) collective-permute-start(f32[128,512]{1,0:T(8,128)S(1)} %get-tuple-element.42), channel_id=1, source_target_pairs={{0,1},{1,0},{2,3},{3,2},{4,5},{5,4},{6,7},{7,6},{8,9},{9,8},{10,11... | collective-permute-start | bytes 786440 | tf_op jit(solution)/shard_map/ppermute | solution.py:264
  16.2 0.0 collective-permute-done.5
  16.3 1.6 %collective-permute-start.6 = (f32[128,512]{1,0:T(8,128)S(1)}, f32[128,512]{1,0:T(8,128)S(1)}, u32[]{:S(2)}, u32[]{:S(2)}) collective-permute-start(f32[128,512]{1,0:T(8,128)S(1)} %add.55), channel_id=1, source_target_pairs={{0,2},{1,3},{2,0},{3,1},{4,6},{5,7},{6,4},{7,5},{8,10},{9,11},{10,... | collective-permute-start | bytes 786440 | tf_op jit(solution)/shard_map/ppermute | solution.py:264
  17.9 6.5 %shard_map.66 = (f32[128,512]{1,0:T(8,128)S(1)}, f32[128,512]{1,0:T(8,128)S(1)}, f32[128,512]{1,0:T(8,128)S(1)}, bf16[2,256,3584]{2,1,0:T(8,128)(2,1)S(1)}, bf16...) custom-call(s32[2]{0:T(128)S(1)} %pad_add_fusion.me, ...), custom_call_target="tpu_custom_call", output_to_operand_aliasing={{5}: (5, {}), {6}: (6, {})} | custom-call | flops 1811939328 | bytes 14155776 | tf_op jit(solution)/shard_map/pallas_call | solution.py:140
  24.4 0.6 collective-permute-start
  25.0 0.0 collective-permute-done.1
  25.0 0.1 collective-permute-start.2
  25.1 0.0 copy-start.1
  25.1 0.0 copy-start
  25.2 3.0 %shard_map.67 = (f32[128,512]{1,0:T(8,128)S(1)}, bf16[2,256,3584]{2,1,0:T(8,128)(2,1)S(1)}, bf16[2,256,1024]{2,1,0:T(8,128)(2,1)S(1)}) custom-call(s32[2]{0:T(128)S(1)} %pad_add_fusion.me, bf16[4096,3584]{1,0:T(8,128)(2,1)} %x.7, bf16[4096,1024]{1,0:T(8,128)(2,1)} %g.7, ...), custom_call_target="tpu_custom_call", output_to_operand_aliasing={{1}: (5, {}), {2}: (6, {})} | custom-call | flops 603979776 | bytes 4718592 | tf_op jit(solution)/shard_map/pallas_call | solution.py:140
  28.2 0.8 %collective-permute-done.4 = f32[128,512]{1,0:T(8,128)S(1)} collective-permute-done((f32[128,512]{1,0:T(8,128)S(1)}, f32[128,512]{1,0:T(8,128)S(1)}, u32[]{:S(2)}, u32[]{:S(2)}) %collective-permute-start.4) | collective-permute-done | bytes 262176 | tf_op jit(solution)/shard_map/ppermute | solution.py:264
  29.0 0.0 collective-permute-done.6
  29.0 0.1 add_add_fusion.own
  29.1 2.7 %collective-permute-start.7 = (f32[96,512]{1,0:T(8,128)S(1)}, f32[96,512]{1,0:T(8,128)S(1)}, u32[]{:S(2)}, u32[]{:S(2)}) collective-permute-start(f32[96,512]{1,0:T(8,128)S(1)} %slice.43), channel_id=1, source_target_pairs={{0,4},{1,5},{2,6},{3,7},{4,0},{5,1},{6,2},{7,3},{8,12},{9,13},{10,... | collective-permute-start | bytes 589832 | tf_op jit(solution)/shard_map/ppermute | solution.py:264
  31.7 1.5 %collective-permute-done = f32[128,512]{1,0:T(8,128)S(1)} collective-permute-done((f32[128,512]{1,0:T(8,128)S(1)}, f32[128,512]{1,0:T(8,128)S(1)}, u32[]{:S(2)}, u32[]{:S(2)}) %collective-permute-start) | collective-permute-done | bytes 262176 | tf_op jit(solution)/shard_map/ppermute | solution.py:264
  33.2 0.9 %collective-permute-done.2 = f32[128,512]{1,0:T(8,128)S(1)} collective-permute-done((f32[128,512]{1,0:T(8,128)S(1)}, f32[128,512]{1,0:T(8,128)S(1)}, u32[]{:S(2)}, u32[]{:S(2)}) %collective-permute-start.2) | collective-permute-done | bytes 262176 | tf_op jit(solution)/shard_map/ppermute | solution.py:264
  34.1 0.1 add_add_fusion.1.own
  34.2 2.4 %collective-permute-start.3 = (f32[96,512]{1,0:T(8,128)S(1)}, f32[96,512]{1,0:T(8,128)S(1)}, u32[]{:S(2)}, u32[]{:S(2)}) collective-permute-start(f32[96,512]{1,0:T(8,128)S(1)} %slice.42), channel_id=1, source_target_pairs={{0,4},{1,5},{2,6},{3,7},{4,0},{5,1},{6,2},{7,3},{8,12},{9,13},{10,... | collective-permute-start | bytes 589832 | tf_op jit(solution)/shard_map/ppermute | solution.py:264
  36.6 7.6 %collective-permute-done.7.recv = f32[96,512]{1,0:T(8,128)S(1)} collective-permute-done((f32[96,512]{1,0:T(8,128)S(1)}, f32[96,512]{1,0:T(8,128)S(1)}, u32[]{:S(2)}, u32[]{:S(2)}) %collective-permute-start.7) | collective-permute-done | bytes 196640 | tf_op jit(solution)/shard_map/ppermute | solution.py:264
  44.2 0.0 copy-done.1
  44.2 1.0 %shard_map.68 = (f32[2,64,128]{2,1,0:T(8,128)S(1)}, f32[2,64,128]{2,1,0:T(8,128)S(1)}) custom-call(s32[2]{0:T(128)S(1)} %pad_add_fusion.me, s32[16]{0:T(128)S(1)} %copy-done.1, f32[128,512]{1,0:T(8,128)S(1)} %add_add_fusion.own, f32[96,512]{1,0:T(8,128)S(1)} %collective-permute-done.7.recv), custom_call_target="tpu_custom_call" | custom-call | flops 100663296 | bytes 524288 | tf_op jit(solution)/shard_map/pallas_call | solution.py:207
  45.3 2.0 %collective-permute-done.3.recv = f32[96,512]{1,0:T(8,128)S(1)} collective-permute-done((f32[96,512]{1,0:T(8,128)S(1)}, f32[96,512]{1,0:T(8,128)S(1)}, u32[]{:S(2)}, u32[]{:S(2)}) %collective-permute-start.3) | collective-permute-done | bytes 196640 | tf_op jit(solution)/shard_map/ppermute | solution.py:264
  47.3 1.0 %shard_map.69 = (f32[2,64,128]{2,1,0:T(8,128)S(1)}, f32[2,64,128]{2,1,0:T(8,128)S(1)}) custom-call(s32[2]{0:T(128)S(1)} %pad_add_fusion.me, s32[16]{0:T(128)S(1)} %copy-done.1, f32[128,512]{1,0:T(8,128)S(1)} %add_add_fusion.1.own, f32[96,512]{1,0:T(8,128)S(1)} %collective-permute-done.3.recv, f32[2,64,128]{2,1,0:T(8,128)S(1)} %get-tuple-element.45.refs_0_, ...), custom_call_target="tpu_custom_call" | custom-call | flops 100663296 | bytes 524288 | tf_op jit(solution)/shard_map/pallas_call | solution.py:207
  48.3 1.6 %collective-permute-start.8 = (f32[2,64,128]{2,1,0:T(8,128)S(1)}, f32[2,64,128]{2,1,0:T(8,128)S(1)}, u32[]{:S(2)}, u32[]{:S(2)}) collective-permute-start(f32[2,64,128]{2,1,0:T(8,128)S(1)} %get-tuple-element.48), channel_id=1, source_target_pairs={{0,1},{1,0},{2,3},{3,2},{4,5},{5,4},{6,7},{7,6},{8,9},{9,8},{10,11... | collective-permute-start | bytes 196616 | tf_op jit(solution)/shard_map/ppermute | solution.py:264
  49.9 2.7 %collective-permute-done.8 = f32[2,64,128]{2,1,0:T(8,128)S(1)} collective-permute-done((f32[2,64,128]{2,1,0:T(8,128)S(1)}, f32[2,64,128]{2,1,0:T(8,128)S(1)}, u32[]{:S(2)}, u32[]{:S(2)}) %collective-permute-start.8) | collective-permute-done | bytes 65568 | tf_op jit(solution)/shard_map/ppermute | solution.py:264
  52.7 0.1 collective-permute-start.9
  52.7 1.2 %collective-permute-done.9 = f32[2,64,128]{2,1,0:T(8,128)S(1)} collective-permute-done((f32[2,64,128]{2,1,0:T(8,128)S(1)}, f32[2,64,128]{2,1,0:T(8,128)S(1)}, u32[]{:S(2)}, u32[]{:S(2)}) %collective-permute-start.9) | collective-permute-done | bytes 65568 | tf_op jit(solution)/shard_map/ppermute | solution.py:264
  54.0 1.6 %collective-permute-start.11 = (f32[64,128]{1,0:T(8,128)S(1)}, f32[64,128]{1,0:T(8,128)S(1)}, u32[]{:S(2)}, u32[]{:S(2)}) collective-permute-start(f32[64,128]{1,0:T(8,128)S(1)} %get-tuple-element.53), channel_id=1, source_target_pairs={{0,16},{1,17},{2,18},{3,19},{4,20},{5,21},{6,22},{7,23},{8,24},{9,... | collective-permute-start | bytes 98312 | tf_op jit(solution)/shard_map/ppermute | solution.py:283
  55.6 0.6 collective-permute-start.12
  56.2 1.3 %collective-permute-start.10 = (f32[64,128]{1,0:T(8,128)S(1)}, f32[64,128]{1,0:T(8,128)S(1)}, u32[]{:S(2)}, u32[]{:S(2)}) collective-permute-start(f32[64,128]{1,0:T(8,128)S(1)} %get-tuple-element.54), channel_id=1, source_target_pairs={{0,2},{1,3},{2,0},{3,1},{4,6},{5,7},{6,4},{7,5},{8,10},{9,11},{10,... | collective-permute-start | bytes 98312 | tf_op jit(solution)/shard_map/ppermute | solution.py:283
  57.6 0.4 collective-permute-done.11
  58.0 2.5 %collective-permute-done.12 = f32[64,128]{1,0:T(8,128)S(1)} collective-permute-done((f32[64,128]{1,0:T(8,128)S(1)}, f32[64,128]{1,0:T(8,128)S(1)}, u32[]{:S(2)}, u32[]{:S(2)}) %collective-permute-start.12) | collective-permute-done | bytes 32800 | tf_op jit(solution)/shard_map/ppermute | solution.py:283
  60.5 0.0 collective-permute-done.10
  60.5 0.0 copy-done
  60.5 1.0 %score.1 = (f32[4,16,128]{2,1,0:T(8,128)S(1)}, f32[2,16,128]{2,1,0:T(8,128)S(1)}, f32[1,16,128]{2,1,0:T(8,128)S(1)}, f32[1,16,128]{2,1,0:T(8,128)S(1)}) custom-call(s32[2]{0:T(128)S(1)} %pad_add_fusion.me, s32[16]{0:T(128)S(1)} %copy-done.1, f32[64,128]{1,0:T(8,128)S(1)} %add_add_fusion.2.own, bf16[1024,512]{1,0:T(8,128)(2,1)S(1)} %copy-done), custom_call_target="tpu_custom_call" | custom-call | flops 16777216 | bytes 1048576 | tf_op jit(solution)/shard_map/score/pallas_call | solution.py:249
  61.5 1.5 %collective-permute-start.13 = (f32[4,16,128]{2,1,0:T(8,128)S(1)}, f32[4,16,128]{2,1,0:T(8,128)S(1)}, u32[]{:S(2)}, u32[]{:S(2)}) collective-permute-start(f32[4,16,128]{2,1,0:T(8,128)S(1)} %get-tuple-element.50), channel_id=1, source_target_pairs={{0,1},{1,0},{2,3},{3,2},{4,5},{5,4},{6,7},{7,6},{8,9},{9,8},{10,11... | collective-permute-start | bytes 98312 | tf_op jit(solution)/shard_map/ppermute | solution.py:264
  63.0 2.4 %collective-permute-done.13 = f32[4,16,128]{2,1,0:T(8,128)S(1)} collective-permute-done((f32[4,16,128]{2,1,0:T(8,128)S(1)}, f32[4,16,128]{2,1,0:T(8,128)S(1)}, u32[]{:S(2)}, u32[]{:S(2)}) %collective-permute-start.13) | collective-permute-done | bytes 32800 | tf_op jit(solution)/shard_map/ppermute | solution.py:264
  65.5 1.0 %collective-permute-start.14 = (f32[2,16,128]{2,1,0:T(8,128)S(1)}, f32[2,16,128]{2,1,0:T(8,128)S(1)}, u32[]{:S(2)}, u32[]{:S(2)}) collective-permute-start(f32[2,16,128]{2,1,0:T(8,128)S(1)} %slice_add_fusion), channel_id=1, source_target_pairs={{0,2},{1,3},{2,0},{3,1},{4,6},{5,7},{6,4},{7,5},{8,10},{9,11},{10,... | collective-permute-start | bytes 49160 | tf_op jit(solution)/shard_map/ppermute | solution.py:264
  66.5 2.7 %collective-permute-done.14 = f32[2,16,128]{2,1,0:T(8,128)S(1)} collective-permute-done((f32[2,16,128]{2,1,0:T(8,128)S(1)}, f32[2,16,128]{2,1,0:T(8,128)S(1)}, u32[]{:S(2)}, u32[]{:S(2)}) %collective-permute-start.14) | collective-permute-done | bytes 16416 | tf_op jit(solution)/shard_map/ppermute | solution.py:264
  69.2 3.1 %collective-permute-start.15 = (f32[1,16,128]{2,1,0:T(8,128)S(1)}, f32[1,16,128]{2,1,0:T(8,128)S(1)}, u32[]{:S(2)}, u32[]{:S(2)}) collective-permute-start(f32[1,16,128]{2,1,0:T(8,128)S(1)} %slice_add_fusion.1), channel_id=1, source_target_pairs={{0,4},{1,5},{2,6},{3,7},{4,0},{5,1},{6,2},{7,3},{8,12},{9,13},{10,... | collective-permute-start | bytes 24584 | tf_op jit(solution)/shard_map/ppermute | solution.py:264
  72.3 1.6 %collective-permute-done.15 = f32[1,16,128]{2,1,0:T(8,128)S(1)} collective-permute-done((f32[1,16,128]{2,1,0:T(8,128)S(1)}, f32[1,16,128]{2,1,0:T(8,128)S(1)}, u32[]{:S(2)}, u32[]{:S(2)}) %collective-permute-start.15) | collective-permute-done | bytes 8224 | tf_op jit(solution)/shard_map/ppermute | solution.py:264
  73.9 0.6 fusion.1
  (10 shorter events, 0.1 us)
Async XLA Ops:
  4.6 11.7 %collective-permute-start.5 = (f32[128,512]{1,0:T(8,128)S(1)}, f32[128,512]{1,0:T(8,128)S(1)}, u32[]{:S(2)}, u32[]{:S(2)}) collective-permute-start(f32[128,512]{1,0:T(8,128)S(1)} %get-tuple-element.44), channel_id=1, source_target_pairs={{0,1},{1,0},{2,3},{3,2},{4,5},{5,4},{6,7},{7,6},{8,9},{9,8},{10,11... | collective-permute-start | bytes 786440 | tf_op jit(solution)/shard_map/ppermute | solution.py:264
  14.1 10.9 %collective-permute-start.1 = (f32[128,512]{1,0:T(8,128)S(1)}, f32[128,512]{1,0:T(8,128)S(1)}, u32[]{:S(2)}, u32[]{:S(2)}) collective-permute-start(f32[128,512]{1,0:T(8,128)S(1)} %get-tuple-element.40), channel_id=1, source_target_pairs={{0,1},{1,0},{2,3},{3,2},{4,5},{5,4},{6,7},{7,6},{8,9},{9,8},{10,11... | collective-permute-start | bytes 786440 | tf_op jit(solution)/shard_map/ppermute | solution.py:264
  14.2 14.8 %collective-permute-start.4 = (f32[128,512]{1,0:T(8,128)S(1)}, f32[128,512]{1,0:T(8,128)S(1)}, u32[]{:S(2)}, u32[]{:S(2)}) collective-permute-start(f32[128,512]{1,0:T(8,128)S(1)} %get-tuple-element.42), channel_id=1, source_target_pairs={{0,1},{1,0},{2,3},{3,2},{4,5},{5,4},{6,7},{7,6},{8,9},{9,8},{10,11... | collective-permute-start | bytes 786440 | tf_op jit(solution)/shard_map/ppermute | solution.py:264
  16.3 12.7 %collective-permute-start.6 = (f32[128,512]{1,0:T(8,128)S(1)}, f32[128,512]{1,0:T(8,128)S(1)}, u32[]{:S(2)}, u32[]{:S(2)}) collective-permute-start(f32[128,512]{1,0:T(8,128)S(1)} %add.55), channel_id=1, source_target_pairs={{0,2},{1,3},{2,0},{3,1},{4,6},{5,7},{6,4},{7,5},{8,10},{9,11},{10,... | collective-permute-start | bytes 786440 | tf_op jit(solution)/shard_map/ppermute | solution.py:264
  24.4 8.8 %collective-permute-start = (f32[128,512]{1,0:T(8,128)S(1)}, f32[128,512]{1,0:T(8,128)S(1)}, u32[]{:S(2)}, u32[]{:S(2)}) collective-permute-start(f32[128,512]{1,0:T(8,128)S(1)} %get-tuple-element.38), channel_id=1, source_target_pairs={{0,1},{1,0},{2,3},{3,2},{4,5},{5,4},{6,7},{7,6},{8,9},{9,8},{10,11... | collective-permute-start | bytes 786440 | tf_op jit(solution)/shard_map/ppermute | solution.py:264
  25.0 9.1 %collective-permute-start.2 = (f32[128,512]{1,0:T(8,128)S(1)}, f32[128,512]{1,0:T(8,128)S(1)}, u32[]{:S(2)}, u32[]{:S(2)}) collective-permute-start(f32[128,512]{1,0:T(8,128)S(1)} %add.52), channel_id=1, source_target_pairs={{0,2},{1,3},{2,0},{3,1},{4,6},{5,7},{6,4},{7,5},{8,10},{9,11},{10,... | collective-permute-start | bytes 786440 | tf_op jit(solution)/shard_map/ppermute | solution.py:264
  25.1 19.1 %copy-start.1 = (s32[16]{0:T(128)S(1)}, s32[16]{0:T(128)}, u32[]{:S(2)}) copy-start(s32[16]{0:T(128)} %lengths.5) | copy-start | bytes 196
  25.1 35.3 %copy-start = (bf16[1024,512]{1,0:T(8,128)(2,1)S(1)}, bf16[1024,512]{1,0:T(8,128)(2,1)}, u32[]{:S(2)}) copy-start(bf16[1024,512]{1,0:T(8,128)(2,1)} %valid.1) | copy-start | bytes 3145732
  29.1 15.1 %collective-permute-start.7 = (f32[96,512]{1,0:T(8,128)S(1)}, f32[96,512]{1,0:T(8,128)S(1)}, u32[]{:S(2)}, u32[]{:S(2)}) collective-permute-start(f32[96,512]{1,0:T(8,128)S(1)} %slice.43), channel_id=1, source_target_pairs={{0,4},{1,5},{2,6},{3,7},{4,0},{5,1},{6,2},{7,3},{8,12},{9,13},{10,... | collective-permute-start | bytes 589832 | tf_op jit(solution)/shard_map/ppermute | solution.py:264
  34.2 13.1 %collective-permute-start.3 = (f32[96,512]{1,0:T(8,128)S(1)}, f32[96,512]{1,0:T(8,128)S(1)}, u32[]{:S(2)}, u32[]{:S(2)}) collective-permute-start(f32[96,512]{1,0:T(8,128)S(1)} %slice.42), channel_id=1, source_target_pairs={{0,4},{1,5},{2,6},{3,7},{4,0},{5,1},{6,2},{7,3},{8,12},{9,13},{10,... | collective-permute-start | bytes 589832 | tf_op jit(solution)/shard_map/ppermute | solution.py:264
  48.3 4.3 %collective-permute-start.8 = (f32[2,64,128]{2,1,0:T(8,128)S(1)}, f32[2,64,128]{2,1,0:T(8,128)S(1)}, u32[]{:S(2)}, u32[]{:S(2)}) collective-permute-start(f32[2,64,128]{2,1,0:T(8,128)S(1)} %get-tuple-element.48), channel_id=1, source_target_pairs={{0,1},{1,0},{2,3},{3,2},{4,5},{5,4},{6,7},{7,6},{8,9},{9,8},{10,11... | collective-permute-start | bytes 196616 | tf_op jit(solution)/shard_map/ppermute | solution.py:264
  52.7 1.3 %collective-permute-start.9 = (f32[2,64,128]{2,1,0:T(8,128)S(1)}, f32[2,64,128]{2,1,0:T(8,128)S(1)}, u32[]{:S(2)}, u32[]{:S(2)}) collective-permute-start(f32[2,64,128]{2,1,0:T(8,128)S(1)} %add.57), channel_id=1, source_target_pairs={{0,8},{8,0},{16,24},{24,16},{1,9},{9,1},{17,25},{25,17},{2,10},{10... | collective-permute-start | bytes 196616 | tf_op jit(solution)/shard_map/ppermute | solution.py:264
  54.0 4.0 %collective-permute-start.11 = (f32[64,128]{1,0:T(8,128)S(1)}, f32[64,128]{1,0:T(8,128)S(1)}, u32[]{:S(2)}, u32[]{:S(2)}) collective-permute-start(f32[64,128]{1,0:T(8,128)S(1)} %get-tuple-element.53), channel_id=1, source_target_pairs={{0,16},{1,17},{2,18},{3,19},{4,20},{5,21},{6,22},{7,23},{8,24},{9,... | collective-permute-start | bytes 98312 | tf_op jit(solution)/shard_map/ppermute | solution.py:283
  55.6 4.8 %collective-permute-start.12 = (f32[64,128]{1,0:T(8,128)S(1)}, f32[64,128]{1,0:T(8,128)S(1)}, u32[]{:S(2)}, u32[]{:S(2)}) collective-permute-start(f32[64,128]{1,0:T(8,128)S(1)} %get-tuple-element.54), channel_id=1, source_target_pairs={{0,18},{1,19},{2,16},{3,17},{4,22},{5,23},{6,20},{7,21},{8,26},{9,... | collective-permute-start | bytes 98312 | tf_op jit(solution)/shard_map/ppermute | solution.py:283
  56.2 4.2 %collective-permute-start.10 = (f32[64,128]{1,0:T(8,128)S(1)}, f32[64,128]{1,0:T(8,128)S(1)}, u32[]{:S(2)}, u32[]{:S(2)}) collective-permute-start(f32[64,128]{1,0:T(8,128)S(1)} %get-tuple-element.54), channel_id=1, source_target_pairs={{0,2},{1,3},{2,0},{3,1},{4,6},{5,7},{6,4},{7,5},{8,10},{9,11},{10,... | collective-permute-start | bytes 98312 | tf_op jit(solution)/shard_map/ppermute | solution.py:283
  61.5 3.9 %collective-permute-start.13 = (f32[4,16,128]{2,1,0:T(8,128)S(1)}, f32[4,16,128]{2,1,0:T(8,128)S(1)}, u32[]{:S(2)}, u32[]{:S(2)}) collective-permute-start(f32[4,16,128]{2,1,0:T(8,128)S(1)} %get-tuple-element.50), channel_id=1, source_target_pairs={{0,1},{1,0},{2,3},{3,2},{4,5},{5,4},{6,7},{7,6},{8,9},{9,8},{10,11... | collective-permute-start | bytes 98312 | tf_op jit(solution)/shard_map/ppermute | solution.py:264
  65.5 3.7 %collective-permute-start.14 = (f32[2,16,128]{2,1,0:T(8,128)S(1)}, f32[2,16,128]{2,1,0:T(8,128)S(1)}, u32[]{:S(2)}, u32[]{:S(2)}) collective-permute-start(f32[2,16,128]{2,1,0:T(8,128)S(1)} %slice_add_fusion), channel_id=1, source_target_pairs={{0,2},{1,3},{2,0},{3,1},{4,6},{5,7},{6,4},{7,5},{8,10},{9,11},{10,... | collective-permute-start | bytes 49160 | tf_op jit(solution)/shard_map/ppermute | solution.py:264
  69.2 4.7 %collective-permute-start.15 = (f32[1,16,128]{2,1,0:T(8,128)S(1)}, f32[1,16,128]{2,1,0:T(8,128)S(1)}, u32[]{:S(2)}, u32[]{:S(2)}) collective-permute-start(f32[1,16,128]{2,1,0:T(8,128)S(1)} %slice_add_fusion.1), channel_id=1, source_target_pairs={{0,4},{1,5},{2,6},{3,7},{4,0},{5,1},{6,2},{7,3},{8,12},{9,13},{10,... | collective-permute-start | bytes 24584 | tf_op jit(solution)/shard_map/ppermute | solution.py:264

commit v5 on v4

--- a/solution.py
+++ b/solution.py
@@ -218,7 +218,8 @@
     )(me, lengths, own, recv, *prevs)
 
 
-def score_kernel(n_ranks, me, lengths, own, valid, *outs):
+def score_kernel(n_ranks, me, lengths, own, valid, *refs):
+    outs, placed = refs[:-1], refs[-1]
     levels = n_ranks.bit_length() - SCORE_LAST
     prompts = lengths.shape[0]
     turned = own[...].T
@@ -233,10 +234,12 @@
         [turned[i * prompts : (i + 1) * prompts] / count for i in range(lines)], axis=1
     ).astype(jnp.bfloat16)
     width = valid.shape[0] // n_ranks
+    sums = dot_nt(features, valid[...])
+    for s in range(n_ranks):
+        placed[s ^ me[0]] = sums[:, s * width : (s + 1) * width]
     for j in range(n_ranks):
-        start = pl.multiple_of((j ^ me[0]) * width, width)
         level, at = place(j, levels - 1)
-        outs[level][at] = dot_nt(features, valid[pl.ds(start, width), :])
+        outs[level][at] = placed[j]
 
 
 def score(me, lengths, own, valid, n_ranks):
@@ -251,6 +254,7 @@
         in_specs=[smem, smem, vmem, vmem],
         out_specs=[vmem] * levels,
         out_shape=[jax.ShapeDtypeStruct((c, prompts, width), jnp.float32) for c in counts],
+        scratch_shapes=[pltpu.VMEM((n_ranks, prompts, width), jnp.float32)],
         name="score",
         cost_estimate=pl.CostEstimate(
             flops=2 * prompts * valid.size, bytes_accessed=2 * valid.size, transcendentals=0

time: 74.6 us -> 74.7 us (level)
  no operation moved by 1% of the time
where the time goes in v5:
time: 74.7 us; the launch traced here: 74.5 us
  waiting for transfers between devices  26.4 us (35%)
  Pallas kernels  23.6 us (32%)
  starting transfers between devices  23.4 us (31%)
  other arithmetic  0.9 us (1%)
    ppermute x13, waiting for transfers between devices, swap(): return lax.ppermute(value, axis, [(i, i ^ 1 << bit) for i in range(count)])  23.5 us
    pallas_call x4, Pallas kernels, project(): pl.pallas_call(functools.partial(project_kernel, first, n_blocks, here, a...  20.6 us
    ppermute x13, starting transfers between devices, swap(): return lax.ppermute(value, axis, [(i, i ^ 1 << bit) for i in range(count)])  19.8 us
    ppermute x3, starting transfers between devices, direct(): total = total + lax.ppermute(value, ('dp', 'tensor'), pairs)  3.55 us
    ppermute x3, waiting for transfers between devices, direct(): total = total + lax.ppermute(value, ('dp', 'tensor'), pairs)  2.9 us
    pallas_call x2, Pallas kernels, gram(): pl.pallas_call(functools.partial(gram_kernel, n_blocks, here, tok_rows, b...  2.05 us
  transfers between devices with their start and end apart: 16, of which 12 were waited for; matrix products, arithmetic and copies ran while one was open for 0% of the time, Pallas kernels for 23%

profile of v5, /device:TPU:0, one launch (start us, length us, event | category | flops | bytes accessed | tf_op | source)
XLA Modules:
  0.0 74.5 jit_solution(13521703703424257547)
XLA Ops:
  0.0 0.1 pad_add_fusion.me
  0.1 4.5 %shard_map.64 = (f32[128,512]{1,0:T(8,128)S(1)}, bf16[6,256,3584]{2,1,0:T(8,128)(2,1)S(1)}, bf16[6,256,1024]{2,1,0:T(8,128)(2,1)S(1)}, bf16[64,3584]{1,0:T(8,128)(2,1)S(1)}, bf16[64,1024]{1,0:T(8,128)(2,1)S(1)}) custom-call(s32[2]{0:T(128)S(1)} %pad_add_fusion.me, bf16[4096,3584]{1,0:T(8,128)(2,1)} %x.7, bf16[4096,1024]{1,0:T(8,128)(2,1)} %g.7, ...), custom_call_target="tpu_custom_call" | custom-call | flops 603979776 | bytes 4718592 | tf_op jit(solution)/shard_map/pallas_call | solution.py:140
  4.6 3.0 %collective-permute-start.5 = (f32[128,512]{1,0:T(8,128)S(1)}, f32[128,512]{1,0:T(8,128)S(1)}, u32[]{:S(2)}, u32[]{:S(2)}) collective-permute-start(f32[128,512]{1,0:T(8,128)S(1)} %get-tuple-element.44), channel_id=1, source_target_pairs={{0,1},{1,0},{2,3},{3,2},{4,5},{5,4},{6,7},{7,6},{8,9},{9,8},{10,11... | collective-permute-start | bytes 786440 | tf_op jit(solution)/shard_map/ppermute | solution.py:268
  7.6 6.5 %shard_map.65 = (f32[128,512]{1,0:T(8,128)S(1)}, f32[128,512]{1,0:T(8,128)S(1)}, f32[128,512]{1,0:T(8,128)S(1)}, bf16[6,256,3584]{2,1,0:T(8,128)(2,1)S(1)}, bf16...) custom-call(s32[2]{0:T(128)S(1)} %pad_add_fusion.me, ...), custom_call_target="tpu_custom_call", output_to_operand_aliasing={{5}: (5, {}), {6}: (6, {})} | custom-call | flops 1811939328 | bytes 14155776 | tf_op jit(solution)/shard_map/pallas_call | solution.py:140
  14.1 0.1 collective-permute-start.1
  14.2 2.0 %collective-permute-start.4 = (f32[128,512]{1,0:T(8,128)S(1)}, f32[128,512]{1,0:T(8,128)S(1)}, u32[]{:S(2)}, u32[]{:S(2)}) collective-permute-start(f32[128,512]{1,0:T(8,128)S(1)} %get-tuple-element.42), channel_id=1, source_target_pairs={{0,1},{1,0},{2,3},{3,2},{4,5},{5,4},{6,7},{7,6},{8,9},{9,8},{10,11... | collective-permute-start | bytes 786440 | tf_op jit(solution)/shard_map/ppermute | solution.py:268
  16.2 0.0 collective-permute-done.5
  16.3 1.6 %collective-permute-start.6 = (f32[128,512]{1,0:T(8,128)S(1)}, f32[128,512]{1,0:T(8,128)S(1)}, u32[]{:S(2)}, u32[]{:S(2)}) collective-permute-start(f32[128,512]{1,0:T(8,128)S(1)} %add.55), channel_id=1, source_target_pairs={{0,2},{1,3},{2,0},{3,1},{4,6},{5,7},{6,4},{7,5},{8,10},{9,11},{10,... | collective-permute-start | bytes 786440 | tf_op jit(solution)/shard_map/ppermute | solution.py:268
  17.9 6.5 %shard_map.66 = (f32[128,512]{1,0:T(8,128)S(1)}, f32[128,512]{1,0:T(8,128)S(1)}, f32[128,512]{1,0:T(8,128)S(1)}, bf16[2,256,3584]{2,1,0:T(8,128)(2,1)S(1)}, bf16...) custom-call(s32[2]{0:T(128)S(1)} %pad_add_fusion.me, ...), custom_call_target="tpu_custom_call", output_to_operand_aliasing={{5}: (5, {}), {6}: (6, {})} | custom-call | flops 1811939328 | bytes 14155776 | tf_op jit(solution)/shard_map/pallas_call | solution.py:140
  24.4 0.6 collective-permute-start
  25.0 0.0 collective-permute-done.1
  25.0 0.1 collective-permute-start.2
  25.1 0.0 copy-start.1
  25.1 0.0 copy-start
  25.2 3.0 %shard_map.67 = (f32[128,512]{1,0:T(8,128)S(1)}, bf16[2,256,3584]{2,1,0:T(8,128)(2,1)S(1)}, bf16[2,256,1024]{2,1,0:T(8,128)(2,1)S(1)}) custom-call(s32[2]{0:T(128)S(1)} %pad_add_fusion.me, bf16[4096,3584]{1,0:T(8,128)(2,1)} %x.7, bf16[4096,1024]{1,0:T(8,128)(2,1)} %g.7, ...), custom_call_target="tpu_custom_call", output_to_operand_aliasing={{1}: (5, {}), {2}: (6, {})} | custom-call | flops 603979776 | bytes 4718592 | tf_op jit(solution)/shard_map/pallas_call | solution.py:140
  28.2 0.8 %collective-permute-done.4 = f32[128,512]{1,0:T(8,128)S(1)} collective-permute-done((f32[128,512]{1,0:T(8,128)S(1)}, f32[128,512]{1,0:T(8,128)S(1)}, u32[]{:S(2)}, u32[]{:S(2)}) %collective-permute-start.4) | collective-permute-done | bytes 262176 | tf_op jit(solution)/shard_map/ppermute | solution.py:268
  29.0 0.0 collective-permute-done.6
  29.0 0.1 add_add_fusion.own
  29.1 2.7 %collective-permute-start.7 = (f32[96,512]{1,0:T(8,128)S(1)}, f32[96,512]{1,0:T(8,128)S(1)}, u32[]{:S(2)}, u32[]{:S(2)}) collective-permute-start(f32[96,512]{1,0:T(8,128)S(1)} %slice.43), channel_id=1, source_target_pairs={{0,4},{1,5},{2,6},{3,7},{4,0},{5,1},{6,2},{7,3},{8,12},{9,13},{10,... | collective-permute-start | bytes 589832 | tf_op jit(solution)/shard_map/ppermute | solution.py:268
  31.7 1.5 %collective-permute-done = f32[128,512]{1,0:T(8,128)S(1)} collective-permute-done((f32[128,512]{1,0:T(8,128)S(1)}, f32[128,512]{1,0:T(8,128)S(1)}, u32[]{:S(2)}, u32[]{:S(2)}) %collective-permute-start) | collective-permute-done | bytes 262176 | tf_op jit(solution)/shard_map/ppermute | solution.py:268
  33.2 0.9 %collective-permute-done.2 = f32[128,512]{1,0:T(8,128)S(1)} collective-permute-done((f32[128,512]{1,0:T(8,128)S(1)}, f32[128,512]{1,0:T(8,128)S(1)}, u32[]{:S(2)}, u32[]{:S(2)}) %collective-permute-start.2) | collective-permute-done | bytes 262176 | tf_op jit(solution)/shard_map/ppermute | solution.py:268
  34.1 0.1 add_add_fusion.1.own
  34.2 2.4 %collective-permute-start.3 = (f32[96,512]{1,0:T(8,128)S(1)}, f32[96,512]{1,0:T(8,128)S(1)}, u32[]{:S(2)}, u32[]{:S(2)}) collective-permute-start(f32[96,512]{1,0:T(8,128)S(1)} %slice.42), channel_id=1, source_target_pairs={{0,4},{1,5},{2,6},{3,7},{4,0},{5,1},{6,2},{7,3},{8,12},{9,13},{10,... | collective-permute-start | bytes 589832 | tf_op jit(solution)/shard_map/ppermute | solution.py:268
  36.6 7.6 %collective-permute-done.7.recv = f32[96,512]{1,0:T(8,128)S(1)} collective-permute-done((f32[96,512]{1,0:T(8,128)S(1)}, f32[96,512]{1,0:T(8,128)S(1)}, u32[]{:S(2)}, u32[]{:S(2)}) %collective-permute-start.7) | collective-permute-done | bytes 196640 | tf_op jit(solution)/shard_map/ppermute | solution.py:268
  44.2 0.0 copy-done.1
  44.2 1.0 %shard_map.68 = (f32[2,64,128]{2,1,0:T(8,128)S(1)}, f32[2,64,128]{2,1,0:T(8,128)S(1)}) custom-call(s32[2]{0:T(128)S(1)} %pad_add_fusion.me, s32[16]{0:T(128)S(1)} %copy-done.1, f32[128,512]{1,0:T(8,128)S(1)} %add_add_fusion.own, f32[96,512]{1,0:T(8,128)S(1)} %collective-permute-done.7.recv), custom_call_target="tpu_custom_call" | custom-call | flops 100663296 | bytes 524288 | tf_op jit(solution)/shard_map/pallas_call | solution.py:207
  45.3 2.0 %collective-permute-done.3.recv = f32[96,512]{1,0:T(8,128)S(1)} collective-permute-done((f32[96,512]{1,0:T(8,128)S(1)}, f32[96,512]{1,0:T(8,128)S(1)}, u32[]{:S(2)}, u32[]{:S(2)}) %collective-permute-start.3) | collective-permute-done | bytes 196640 | tf_op jit(solution)/shard_map/ppermute | solution.py:268
  47.3 1.0 %shard_map.69 = (f32[2,64,128]{2,1,0:T(8,128)S(1)}, f32[2,64,128]{2,1,0:T(8,128)S(1)}) custom-call(s32[2]{0:T(128)S(1)} %pad_add_fusion.me, s32[16]{0:T(128)S(1)} %copy-done.1, f32[128,512]{1,0:T(8,128)S(1)} %add_add_fusion.1.own, f32[96,512]{1,0:T(8,128)S(1)} %collective-permute-done.3.recv, f32[2,64,128]{2,1,0:T(8,128)S(1)} %get-tuple-element.45.refs_0_, ...), custom_call_target="tpu_custom_call" | custom-call | flops 100663296 | bytes 524288 | tf_op jit(solution)/shard_map/pallas_call | solution.py:207
  48.3 1.6 %collective-permute-start.8 = (f32[2,64,128]{2,1,0:T(8,128)S(1)}, f32[2,64,128]{2,1,0:T(8,128)S(1)}, u32[]{:S(2)}, u32[]{:S(2)}) collective-permute-start(f32[2,64,128]{2,1,0:T(8,128)S(1)} %get-tuple-element.48), channel_id=1, source_target_pairs={{0,1},{1,0},{2,3},{3,2},{4,5},{5,4},{6,7},{7,6},{8,9},{9,8},{10,11... | collective-permute-start | bytes 196616 | tf_op jit(solution)/shard_map/ppermute | solution.py:268
  49.9 2.7 %collective-permute-done.8 = f32[2,64,128]{2,1,0:T(8,128)S(1)} collective-permute-done((f32[2,64,128]{2,1,0:T(8,128)S(1)}, f32[2,64,128]{2,1,0:T(8,128)S(1)}, u32[]{:S(2)}, u32[]{:S(2)}) %collective-permute-start.8) | collective-permute-done | bytes 65568 | tf_op jit(solution)/shard_map/ppermute | solution.py:268
  52.7 0.1 collective-permute-start.9
  52.7 1.2 %collective-permute-done.9 = f32[2,64,128]{2,1,0:T(8,128)S(1)} collective-permute-done((f32[2,64,128]{2,1,0:T(8,128)S(1)}, f32[2,64,128]{2,1,0:T(8,128)S(1)}, u32[]{:S(2)}, u32[]{:S(2)}) %collective-permute-start.9) | collective-permute-done | bytes 65568 | tf_op jit(solution)/shard_map/ppermute | solution.py:268
  54.0 1.6 %collective-permute-start.11 = (f32[64,128]{1,0:T(8,128)S(1)}, f32[64,128]{1,0:T(8,128)S(1)}, u32[]{:S(2)}, u32[]{:S(2)}) collective-permute-start(f32[64,128]{1,0:T(8,128)S(1)} %get-tuple-element.53), channel_id=1, source_target_pairs={{0,16},{1,17},{2,18},{3,19},{4,20},{5,21},{6,22},{7,23},{8,24},{9,... | collective-permute-start | bytes 98312 | tf_op jit(solution)/shard_map/ppermute | solution.py:287
  55.6 0.6 collective-permute-start.12
  56.2 1.3 %collective-permute-start.10 = (f32[64,128]{1,0:T(8,128)S(1)}, f32[64,128]{1,0:T(8,128)S(1)}, u32[]{:S(2)}, u32[]{:S(2)}) collective-permute-start(f32[64,128]{1,0:T(8,128)S(1)} %get-tuple-element.54), channel_id=1, source_target_pairs={{0,2},{1,3},{2,0},{3,1},{4,6},{5,7},{6,4},{7,5},{8,10},{9,11},{10,... | collective-permute-start | bytes 98312 | tf_op jit(solution)/shard_map/ppermute | solution.py:287
  57.6 0.4 collective-permute-done.11
  58.0 2.5 %collective-permute-done.12 = f32[64,128]{1,0:T(8,128)S(1)} collective-permute-done((f32[64,128]{1,0:T(8,128)S(1)}, f32[64,128]{1,0:T(8,128)S(1)}, u32[]{:S(2)}, u32[]{:S(2)}) %collective-permute-start.12) | collective-permute-done | bytes 32800 | tf_op jit(solution)/shard_map/ppermute | solution.py:287
  60.5 0.0 collective-permute-done.10
  60.5 0.0 copy-done
  60.5 1.0 %score.1 = (f32[4,16,128]{2,1,0:T(8,128)S(1)}, f32[2,16,128]{2,1,0:T(8,128)S(1)}, f32[1,16,128]{2,1,0:T(8,128)S(1)}, f32[1,16,128]{2,1,0:T(8,128)S(1)}) custom-call(s32[2]{0:T(128)S(1)} %pad_add_fusion.me, s32[16]{0:T(128)S(1)} %copy-done.1, f32[64,128]{1,0:T(8,128)S(1)} %add_add_fusion.2.own, bf16[1024,512]{1,0:T(8,128)(2,1)S(1)} %copy-done), custom_call_target="tpu_custom_call" | custom-call | flops 16777216 | bytes 1048576 | tf_op jit(solution)/shard_map/score/pallas_call | solution.py:252
  61.5 1.6 %collective-permute-start.13 = (f32[4,16,128]{2,1,0:T(8,128)S(1)}, f32[4,16,128]{2,1,0:T(8,128)S(1)}, u32[]{:S(2)}, u32[]{:S(2)}) collective-permute-start(f32[4,16,128]{2,1,0:T(8,128)S(1)} %get-tuple-element.50), channel_id=1, source_target_pairs={{0,1},{1,0},{2,3},{3,2},{4,5},{5,4},{6,7},{7,6},{8,9},{9,8},{10,11... | collective-permute-start | bytes 98312 | tf_op jit(solution)/shard_map/ppermute | solution.py:268
  63.1 2.4 %collective-permute-done.13 = f32[4,16,128]{2,1,0:T(8,128)S(1)} collective-permute-done((f32[4,16,128]{2,1,0:T(8,128)S(1)}, f32[4,16,128]{2,1,0:T(8,128)S(1)}, u32[]{:S(2)}, u32[]{:S(2)}) %collective-permute-start.13) | collective-permute-done | bytes 32800 | tf_op jit(solution)/shard_map/ppermute | solution.py:268
  65.5 1.0 %collective-permute-start.14 = (f32[2,16,128]{2,1,0:T(8,128)S(1)}, f32[2,16,128]{2,1,0:T(8,128)S(1)}, u32[]{:S(2)}, u32[]{:S(2)}) collective-permute-start(f32[2,16,128]{2,1,0:T(8,128)S(1)} %slice_add_fusion), channel_id=1, source_target_pairs={{0,2},{1,3},{2,0},{3,1},{4,6},{5,7},{6,4},{7,5},{8,10},{9,11},{10,... | collective-permute-start | bytes 49160 | tf_op jit(solution)/shard_map/ppermute | solution.py:268
  66.5 2.7 %collective-permute-done.14 = f32[2,16,128]{2,1,0:T(8,128)S(1)} collective-permute-done((f32[2,16,128]{2,1,0:T(8,128)S(1)}, f32[2,16,128]{2,1,0:T(8,128)S(1)}, u32[]{:S(2)}, u32[]{:S(2)}) %collective-permute-start.14) | collective-permute-done | bytes 16416 | tf_op jit(solution)/shard_map/ppermute | solution.py:268
  69.2 3.1 %collective-permute-start.15 = (f32[1,16,128]{2,1,0:T(8,128)S(1)}, f32[1,16,128]{2,1,0:T(8,128)S(1)}, u32[]{:S(2)}, u32[]{:S(2)}) collective-permute-start(f32[1,16,128]{2,1,0:T(8,128)S(1)} %slice_add_fusion.1), channel_id=1, source_target_pairs={{0,4},{1,5},{2,6},{3,7},{4,0},{5,1},{6,2},{7,3},{8,12},{9,13},{10,... | collective-permute-start | bytes 24584 | tf_op jit(solution)/shard_map/ppermute | solution.py:268
  72.3 1.6 %collective-permute-done.15 = f32[1,16,128]{2,1,0:T(8,128)S(1)} collective-permute-done((f32[1,16,128]{2,1,0:T(8,128)S(1)}, f32[1,16,128]{2,1,0:T(8,128)S(1)}, u32[]{:S(2)}, u32[]{:S(2)}) %collective-permute-start.15) | collective-permute-done | bytes 8224 | tf_op jit(solution)/shard_map/ppermute | solution.py:268
  73.9 0.6 fusion.1
  (10 shorter events, 0.1 us)
Async XLA Ops:
  4.6 11.7 %collective-permute-start.5 = (f32[128,512]{1,0:T(8,128)S(1)}, f32[128,512]{1,0:T(8,128)S(1)}, u32[]{:S(2)}, u32[]{:S(2)}) collective-permute-start(f32[128,512]{1,0:T(8,128)S(1)} %get-tuple-element.44), channel_id=1, source_target_pairs={{0,1},{1,0},{2,3},{3,2},{4,5},{5,4},{6,7},{7,6},{8,9},{9,8},{10,11... | collective-permute-start | bytes 786440 | tf_op jit(solution)/shard_map/ppermute | solution.py:268
  14.1 10.9 %collective-permute-start.1 = (f32[128,512]{1,0:T(8,128)S(1)}, f32[128,512]{1,0:T(8,128)S(1)}, u32[]{:S(2)}, u32[]{:S(2)}) collective-permute-start(f32[128,512]{1,0:T(8,128)S(1)} %get-tuple-element.40), channel_id=1, source_target_pairs={{0,1},{1,0},{2,3},{3,2},{4,5},{5,4},{6,7},{7,6},{8,9},{9,8},{10,11... | collective-permute-start | bytes 786440 | tf_op jit(solution)/shard_map/ppermute | solution.py:268
  14.2 14.8 %collective-permute-start.4 = (f32[128,512]{1,0:T(8,128)S(1)}, f32[128,512]{1,0:T(8,128)S(1)}, u32[]{:S(2)}, u32[]{:S(2)}) collective-permute-start(f32[128,512]{1,0:T(8,128)S(1)} %get-tuple-element.42), channel_id=1, source_target_pairs={{0,1},{1,0},{2,3},{3,2},{4,5},{5,4},{6,7},{7,6},{8,9},{9,8},{10,11... | collective-permute-start | bytes 786440 | tf_op jit(solution)/shard_map/ppermute | solution.py:268
  16.3 12.7 %collective-permute-start.6 = (f32[128,512]{1,0:T(8,128)S(1)}, f32[128,512]{1,0:T(8,128)S(1)}, u32[]{:S(2)}, u32[]{:S(2)}) collective-permute-start(f32[128,512]{1,0:T(8,128)S(1)} %add.55), channel_id=1, source_target_pairs={{0,2},{1,3},{2,0},{3,1},{4,6},{5,7},{6,4},{7,5},{8,10},{9,11},{10,... | collective-permute-start | bytes 786440 | tf_op jit(solution)/shard_map/ppermute | solution.py:268
  24.4 8.8 %collective-permute-start = (f32[128,512]{1,0:T(8,128)S(1)}, f32[128,512]{1,0:T(8,128)S(1)}, u32[]{:S(2)}, u32[]{:S(2)}) collective-permute-start(f32[128,512]{1,0:T(8,128)S(1)} %get-tuple-element.38), channel_id=1, source_target_pairs={{0,1},{1,0},{2,3},{3,2},{4,5},{5,4},{6,7},{7,6},{8,9},{9,8},{10,11... | collective-permute-start | bytes 786440 | tf_op jit(solution)/shard_map/ppermute | solution.py:268
  25.0 9.1 %collective-permute-start.2 = (f32[128,512]{1,0:T(8,128)S(1)}, f32[128,512]{1,0:T(8,128)S(1)}, u32[]{:S(2)}, u32[]{:S(2)}) collective-permute-start(f32[128,512]{1,0:T(8,128)S(1)} %add.52), channel_id=1, source_target_pairs={{0,2},{1,3},{2,0},{3,1},{4,6},{5,7},{6,4},{7,5},{8,10},{9,11},{10,... | collective-permute-start | bytes 786440 | tf_op jit(solution)/shard_map/ppermute | solution.py:268
  25.1 19.1 %copy-start.1 = (s32[16]{0:T(128)S(1)}, s32[16]{0:T(128)}, u32[]{:S(2)}) copy-start(s32[16]{0:T(128)} %lengths.5) | copy-start | bytes 196
  25.1 35.3 %copy-start = (bf16[1024,512]{1,0:T(8,128)(2,1)S(1)}, bf16[1024,512]{1,0:T(8,128)(2,1)}, u32[]{:S(2)}) copy-start(bf16[1024,512]{1,0:T(8,128)(2,1)} %valid.1) | copy-start | bytes 3145732
  29.1 15.1 %collective-permute-start.7 = (f32[96,512]{1,0:T(8,128)S(1)}, f32[96,512]{1,0:T(8,128)S(1)}, u32[]{:S(2)}, u32[]{:S(2)}) collective-permute-start(f32[96,512]{1,0:T(8,128)S(1)} %slice.43), channel_id=1, source_target_pairs={{0,4},{1,5},{2,6},{3,7},{4,0},{5,1},{6,2},{7,3},{8,12},{9,13},{10,... | collective-permute-start | bytes 589832 | tf_op jit(solution)/shard_map/ppermute | solution.py:268
  34.2 13.1 %collective-permute-start.3 = (f32[96,512]{1,0:T(8,128)S(1)}, f32[96,512]{1,0:T(8,128)S(1)}, u32[]{:S(2)}, u32[]{:S(2)}) collective-permute-start(f32[96,512]{1,0:T(8,128)S(1)} %slice.42), channel_id=1, source_target_pairs={{0,4},{1,5},{2,6},{3,7},{4,0},{5,1},{6,2},{7,3},{8,12},{9,13},{10,... | collective-permute-start | bytes 589832 | tf_op jit(solution)/shard_map/ppermute | solution.py:268
  48.3 4.3 %collective-permute-start.8 = (f32[2,64,128]{2,1,0:T(8,128)S(1)}, f32[2,64,128]{2,1,0:T(8,128)S(1)}, u32[]{:S(2)}, u32[]{:S(2)}) collective-permute-start(f32[2,64,128]{2,1,0:T(8,128)S(1)} %get-tuple-element.48), channel_id=1, source_target_pairs={{0,1},{1,0},{2,3},{3,2},{4,5},{5,4},{6,7},{7,6},{8,9},{9,8},{10,11... | collective-permute-start | bytes 196616 | tf_op jit(solution)/shard_map/ppermute | solution.py:268
  52.7 1.3 %collective-permute-start.9 = (f32[2,64,128]{2,1,0:T(8,128)S(1)}, f32[2,64,128]{2,1,0:T(8,128)S(1)}, u32[]{:S(2)}, u32[]{:S(2)}) collective-permute-start(f32[2,64,128]{2,1,0:T(8,128)S(1)} %add.57), channel_id=1, source_target_pairs={{0,8},{8,0},{16,24},{24,16},{1,9},{9,1},{17,25},{25,17},{2,10},{10... | collective-permute-start | bytes 196616 | tf_op jit(solution)/shard_map/ppermute | solution.py:268
  54.0 4.0 %collective-permute-start.11 = (f32[64,128]{1,0:T(8,128)S(1)}, f32[64,128]{1,0:T(8,128)S(1)}, u32[]{:S(2)}, u32[]{:S(2)}) collective-permute-start(f32[64,128]{1,0:T(8,128)S(1)} %get-tuple-element.53), channel_id=1, source_target_pairs={{0,16},{1,17},{2,18},{3,19},{4,20},{5,21},{6,22},{7,23},{8,24},{9,... | collective-permute-start | bytes 98312 | tf_op jit(solution)/shard_map/ppermute | solution.py:287
  55.6 4.8 %collective-permute-start.12 = (f32[64,128]{1,0:T(8,128)S(1)}, f32[64,128]{1,0:T(8,128)S(1)}, u32[]{:S(2)}, u32[]{:S(2)}) collective-permute-start(f32[64,128]{1,0:T(8,128)S(1)} %get-tuple-element.54), channel_id=1, source_target_pairs={{0,18},{1,19},{2,16},{3,17},{4,22},{5,23},{6,20},{7,21},{8,26},{9,... | collective-permute-start | bytes 98312 | tf_op jit(solution)/shard_map/ppermute | solution.py:287
  56.2 4.2 %collective-permute-start.10 = (f32[64,128]{1,0:T(8,128)S(1)}, f32[64,128]{1,0:T(8,128)S(1)}, u32[]{:S(2)}, u32[]{:S(2)}) collective-permute-start(f32[64,128]{1,0:T(8,128)S(1)} %get-tuple-element.54), channel_id=1, source_target_pairs={{0,2},{1,3},{2,0},{3,1},{4,6},{5,7},{6,4},{7,5},{8,10},{9,11},{10,... | collective-permute-start | bytes 98312 | tf_op jit(solution)/shard_map/ppermute | solution.py:287
  61.5 4.0 %collective-permute-start.13 = (f32[4,16,128]{2,1,0:T(8,128)S(1)}, f32[4,16,128]{2,1,0:T(8,128)S(1)}, u32[]{:S(2)}, u32[]{:S(2)}) collective-permute-start(f32[4,16,128]{2,1,0:T(8,128)S(1)} %get-tuple-element.50), channel_id=1, source_target_pairs={{0,1},{1,0},{2,3},{3,2},{4,5},{5,4},{6,7},{7,6},{8,9},{9,8},{10,11... | collective-permute-start | bytes 98312 | tf_op jit(solution)/shard_map/ppermute | solution.py:268
  65.5 3.7 %collective-permute-start.14 = (f32[2,16,128]{2,1,0:T(8,128)S(1)}, f32[2,16,128]{2,1,0:T(8,128)S(1)}, u32[]{:S(2)}, u32[]{:S(2)}) collective-permute-start(f32[2,16,128]{2,1,0:T(8,128)S(1)} %slice_add_fusion), channel_id=1, source_target_pairs={{0,2},{1,3},{2,0},{3,1},{4,6},{5,7},{6,4},{7,5},{8,10},{9,11},{10,... | collective-permute-start | bytes 49160 | tf_op jit(solution)/shard_map/ppermute | solution.py:268
  69.2 4.7 %collective-permute-start.15 = (f32[1,16,128]{2,1,0:T(8,128)S(1)}, f32[1,16,128]{2,1,0:T(8,128)S(1)}, u32[]{:S(2)}, u32[]{:S(2)}) collective-permute-start(f32[1,16,128]{2,1,0:T(8,128)S(1)} %slice_add_fusion.1), channel_id=1, source_target_pairs={{0,4},{1,5},{2,6},{3,7},{4,0},{5,1},{6,2},{7,3},{8,12},{9,13},{10,... | collective-permute-start | bytes 24584 | tf_op jit(solution)/shard_map/ppermute | solution.py:268
